TPU v7x, 32 devices: a whole 2x2x4 slice. The times are simulated.
32 devices in a mesh: grp: 2 (over y), row: 8 (over z, core), col: 2 (over x), ch: 1.
Axes of the slice: x: 2, y: 2, z: 4, core: 2. Of those that a mesh axis runs over, the one named last changes fastest.
Arguments:
- maps: bfloat16 [64, 512, 256], P('ch', ('grp', 'row'), 'col'), parts along dimension 1, may hold values from -6 to 6
- weights: bfloat16 [6, 3, 3, 64, 64], P(None, None, None, 'ch'), may hold values from -0.25 to 0.25
- biases: bfloat16 [6, 64], P(None, 'ch'), may hold values from -3 to 3
- dilations: int32 [6], replicated, may hold values from 1 to 8, as said below
Outputs:
- decoded: bfloat16 [64, 512, 256], P('ch', ('grp', 'row'), 'col'), parts along dimension 1
There are 2 independent parts, one for each index of `grp`. A program takes and returns all parts, laid end to end along the dimension named above; an argument that names none is the same for every part. Nothing has to cross between parts.
Inputs may be any that keep to these rules, and one draw needn't show every extreme that they name: `dilations`: each dilation is a power of two; some layer has dilation 8.
All inputs are finite; a program needn't handle non-finite values.
Results may differ from a plain program's by a relative error of at most 0.0061.
Values may be sent and summed in bfloat16 or wider, within the bound.
No kernel may reach another device: no remote copies, remote signals or barrier semaphores. Data moves between devices by JAX's collectives and lax.ppermute only.
A program may use at most 64 MiB of HBM per device.

v0:
```python
import functools

import jax
import jax.numpy as jnp
from jax import lax
from jax.experimental import pallas as pl
from jax.experimental.pallas import tpu as pltpu
from jax.sharding import PartitionSpec as P

LAYERS = 6
DMAX = 8


def extended(block, sides, width):
    for axis, dim in sides:
        count = lax.axis_size(axis)
        forward = [(i, i + 1) for i in range(count - 1)]
        backward = [(target, source) for source, target in forward]
        low = lax.ppermute(
            lax.slice_in_dim(block, block.shape[dim] - width, None, axis=dim), axis, forward
        )
        high = lax.ppermute(lax.slice_in_dim(block, 0, width, axis=dim), axis, backward)
        block = jnp.concatenate([low, block, high], axis=dim)
    return block


def contribution(piece, weight_piece, spacing, row_count, col_count):
    count = piece.shape[0]
    out_count = weight_piece.shape[2]
    matrix = jnp.transpose(weight_piece, (2, 0, 1, 3)).reshape(out_count, 9 * count)
    block = 128
    results = []
    for block_index in range(col_count // block):
        windows = []
        for tap_row in range(3):
            for tap_col in range(3):
                row_start = DMAX + (tap_row - 1) * spacing
                col_start = DMAX + (tap_col - 1) * spacing + block_index * block
                windows.append(
                    lax.dynamic_slice(
                        piece, (jnp.int32(0), row_start, col_start), (count, row_count, block)
                    )
                )
        stacked = jnp.stack(windows, 0).reshape(9 * count, row_count * block)
        product = jnp.dot(matrix, stacked, preferred_element_type=jnp.float32)
        results.append(product.reshape(out_count, row_count, block))
    return jnp.concatenate(results, axis=2)


def finish(current, summed, tap_bias):
    branch = jax.nn.gelu(summed + tap_bias[:, None, None].astype(jnp.float32), approximate=False)
    return (current.astype(jnp.float32) + branch).astype(jnp.bfloat16)


def conv_whole(current, padded, tap_weights, tap_bias, spacing):
    summed = contribution(padded, tap_weights, spacing, current.shape[1], current.shape[2])
    return finish(current, summed, tap_bias)


def to_slab(current):
    return lax.all_to_all(current, "col", split_axis=1, concat_axis=2, tiled=True)


def to_tile(current):
    return lax.all_to_all(current, "col", split_axis=2, concat_axis=1, tiled=True)


def split_rows(current):
    return lax.all_to_all(current, "ch", split_axis=1, concat_axis=0, tiled=True)


def join_rows(current):
    return lax.all_to_all(current, "ch", split_axis=0, concat_axis=1, tiled=True)


def mirror(slab):
    flipped = jnp.swapaxes(slab, 1, 2)
    other = lax.all_to_all(flipped, ("row", "col"), split_axis=1, concat_axis=2, tiled=True)
    return (0.5 * (slab.astype(jnp.float32) + other.astype(jnp.float32))).astype(jnp.bfloat16)


def on_device(maps, weights, biases, dilations):
    layers_n = weights.shape[0]
    bias_block = biases.reshape(layers_n, 1, 1, biases.shape[1], 1)
    full_weights, full_bias = (
        lax.all_gather(weights, "ch", axis=3, tiled=True),
        lax.all_gather(bias_block, "ch", axis=3, tiled=True),
    )
    full_bias = full_bias.reshape(layers_n, full_bias.shape[3])
    current = split_rows(maps)
    for layer in range(LAYERS):
        padded = extended(current, ((("row", "ch"), 1), ("col", 2)), DMAX)
        current = conv_whole(
            current, padded, full_weights[layer], full_bias[layer], dilations[layer]
        )
        if layer == LAYERS // 2 - 1:
            current = split_rows(to_tile(mirror(to_slab(join_rows(current)))))
    return join_rows(current)


CH = 64
ROWS = 32
COLS = 128
HALF = LAYERS // 2
HALO = HALF * DMAX
SLOT = 32
FULL = ROWS + 2 * HALO
KDIM = 3 * CH + 16
UNROLL = 16
BF16 = jnp.bfloat16
F32 = jnp.float32


def place():
    r, c = lax.axis_index("row"), lax.axis_index("col")
    return r, c, lax.rem(r, 2)


def edge_pack(row_of, out_ref, c, start, groups):
    lane = lax.broadcasted_iota(jnp.int32, (CH, COLS), 1)
    for t in range(groups):
        acc = None
        for q in range(4):
            piece = pltpu.roll(row_of(start + t + groups * q), lax.rem(SLOT * (q + 1 - c), COLS), 1)
            acc = piece if acc is None else jnp.where(lane >= SLOT * q, piece, acc)
        out_ref[t] = acc.astype(BF16)


def pack_sends(read, a_ref, b_ref, c_ref, d_ref, e_ref, c, core):
    off_a = (ROWS - HALO) * (1 - core)
    off_b = (ROWS - HALO) * core
    for i in range(HALO):
        a_ref[i] = read(off_a + i)
        b_ref[i] = read(off_b + i)

    def row_of(i):
        return read(i).astype(F32)

    edge_pack(row_of, c_ref, c, 0, ROWS // 4)
    edge_pack(row_of, d_ref, c, off_a, HALO // 4)
    edge_pack(row_of, e_ref, c, off_b, HALO // 4)


def pack_kernel(x_ref, xt_ref, a_ref, b_ref, c_ref, d_ref, e_ref, flat):
    _, c, core = place()
    flat[...] = x_ref[...].reshape(CH * ROWS, COLS).astype(F32)
    for h in range(ROWS):
        xt_ref[h] = flat[pl.ds(h, CH, stride=ROWS), :].astype(BF16)
    pack_sends(lambda i: xt_ref[i], a_ref, b_ref, c_ref, d_ref, e_ref, c, core)


def assemble(xa, xt_ref, a_ref, b_ref, c_ref, d_ref, e_ref, c, core):
    lane = lax.broadcasted_iota(jnp.int32, (CH, COLS), 1)
    first = c * (COLS - SLOT)
    mask = (lane >= first) & (lane < first + SLOT)
    at_a = (FULL - HALO) * (1 - core)
    at_b = (FULL - HALO) * core
    for i in range(ROWS):
        xa[HALO + i, :, 0:COLS] = xt_ref[i]
    for i in range(HALO):
        xa[at_a + i, :, 0:COLS] = a_ref[i]
        xa[at_b + i, :, 0:COLS] = b_ref[i]
    for ref, start, groups in ((c_ref, HALO, ROWS // 4), (d_ref, at_a, HALO // 4), (e_ref, at_b, HALO // 4)):
        for t in range(groups):
            packed = ref[t].astype(F32)
            for q in range(4):
                piece = pltpu.roll(packed, lax.rem(COLS + first - SLOT * q, COLS), 1)
                xa[start + t + groups * q, :, COLS:] = jnp.where(mask, piece, 0.0).astype(BF16)
    return mask


def run_layers(base, dil_ref, w_ref, xa, xb, mask, last, row_count):
    r, _, _ = place()
    lo_map = jnp.where(r == 0, HALO, 0)
    hi_map = jnp.where(r == row_count - 1, HALO + ROWS, FULL)
    lane = lax.broadcasted_iota(jnp.int32, (CH, COLS), 1)
    ones = jnp.where(lax.broadcasted_iota(jnp.int32, (16, 2 * COLS), 0) == 0, 1.0, 0.0).astype(BF16)
    zeros = jnp.zeros((CH, 2 * COLS), BF16)
    for i in range(HALO):
        xb[i] = zeros
        xb[FULL - HALO + i] = zeros
    src, dst = xa, xb
    for layer in range(HALF):
        s = dil_ref[base + layer]
        rest = 0
        for later in range(layer + 1, HALF):
            rest = rest + dil_ref[base + later]
        final = layer == HALF - 1
        lo = jnp.maximum(HALO - rest, lo_map) if not final else jnp.int32(HALO)
        hi = jnp.minimum(HALO + ROWS + rest, hi_map) if not final else jnp.int32(HALO + ROWS)
        from_left, from_right = lane >= s, lane < COLS - s

        def row(h, src=src, dst=dst, s=s, layer=layer, fl=from_left, fr=from_right, final=final):
            taps = jnp.concatenate([src[h - s], src[h], src[h + s], ones], axis=0)
            y = jnp.dot(w_ref[layer], taps, preferred_element_type=F32)
            left = [pltpu.roll(y[0:CH, k * COLS : (k + 1) * COLS], s, 1) for k in range(2)]
            right = [pltpu.roll(y[2 * CH :, k * COLS : (k + 1) * COLS], COLS - s, 1) for k in range(2)]
            for k in range(1 if final else 2):
                half = (
                    y[CH : 2 * CH, k * COLS : (k + 1) * COLS]
                    + jnp.where(fl, left[k], left[1 - k])
                    + jnp.where(fr, right[k], right[1 - k])
                )
                branch = half + half * lax.erf(half * 1.4142135623730951)
                new = src[h, :, k * COLS : (k + 1) * COLS].astype(F32) + branch
                if final:
                    last(h - HALO, new)
                elif k == 0:
                    dst[h, :, 0:COLS] = new.astype(BF16)
                else:
                    dst[h, :, COLS:] = jnp.where(mask, new, 0.0).astype(BF16)

        def step(i, _, lo=lo, hi=hi, row=row):
            first = jnp.minimum(lo + i * UNROLL, hi - UNROLL)
            for u in range(UNROLL):
                row(first + u)
            return 0

        lax.fori_loop(0, (hi - lo + UNROLL - 1) // UNROLL, step, 0)
        src, dst = dst, src


def first_kernel(row_count, dil_ref, w_ref, xt_ref, a_ref, b_ref, c_ref, d_ref, e_ref,
                 x_ref, m0, m1, m2, m3, xa, xb, flat, turned):
    r, c, core = place()
    mask = assemble(xa, xt_ref, a_ref, b_ref, c_ref, d_ref, e_ref, c, core)

    def last(h, new):
        rounded = new.astype(BF16)
        x_ref[h] = rounded
        flat[pl.ds(h, CH, stride=ROWS), :] = rounded.astype(F32)

    run_layers(0, dil_ref, w_ref, xa, xb, mask, last, row_count)
    for g in range(16):
        four = jnp.concatenate([flat[(16 * k + g) * ROWS : (16 * k + g + 1) * ROWS, :] for k in range(4)], axis=0)
        turned[pl.ds(g, COLS, stride=16), :] = four.T
    rr = lax.rem(r, 4)
    for k, ref in enumerate((m0, m1, m2, m3)):
        start = pl.multiple_of(jnp.bitwise_xor(rr, k) * (ROWS * 16), ROWS * 16)
        ref[...] = turned[pl.ds(start, ROWS * 16), :].reshape(ROWS, 16, COLS).astype(BF16)


def mirror_kernel(x_ref, m0, m1, m2, m3, xt_ref, a_ref, b_ref, c_ref, d_ref, e_ref, got):
    r, c, core = place()
    rr = lax.rem(r, 4)
    for k, ref in enumerate((m0, m1, m2, m3)):
        got[jnp.bitwise_xor(rr, k)] = ref[...]
    slot = lax.broadcasted_iota(jnp.int32, (16, COLS), 1) // SLOT

    def by_slot(pieces):
        out = pieces[0]
        for q in range(1, 4):
            out = jnp.where(slot >= q, pieces[q], out)
        return out

    for i in range(ROWS):
        parts = [got[q, i].astype(F32) for q in range(4)]
        moved = []
        for d in range(4):
            v = by_slot([parts[(q + d) % 4] for q in range(4)])
            moved.append(pltpu.roll(v, SLOT * d, 1) if d else v)
        mirrored = jnp.concatenate(
            [by_slot([moved[(q - k) % 4] for q in range(4)]) for k in range(4)], axis=0
        )
        xt_ref[i] = (0.5 * (x_ref[i].astype(F32) + mirrored)).astype(BF16)
    pack_sends(lambda i: xt_ref[i], a_ref, b_ref, c_ref, d_ref, e_ref, c, core)


def second_kernel(row_count, dil_ref, w_ref, xt_ref, a_ref, b_ref, c_ref, d_ref, e_ref, o_ref, xa, xb, flat):
    _, c, core = place()
    mask = assemble(xa, xt_ref, a_ref, b_ref, c_ref, d_ref, e_ref, c, core)

    def last(h, new):
        flat[pl.ds(h, CH, stride=ROWS), :] = new

    run_layers(HALF, dil_ref, w_ref, xa, xb, mask, last, row_count)
    o_ref[...] = flat[...].reshape(CH, ROWS, COLS).astype(BF16)


def kernel_call(body, outs, scratch, operands, smem=0, cost=None):
    vmem = pl.BlockSpec(memory_space=pltpu.VMEM)
    return pl.pallas_call(
        body,
        out_shape=[jax.ShapeDtypeStruct(shape, BF16) for shape in outs],
        in_specs=[pl.BlockSpec(memory_space=pltpu.SMEM)] * smem + [vmem] * (len(operands) - smem),
        out_specs=[vmem] * len(outs),
        scratch_shapes=[pltpu.VMEM(shape, dtype) for shape, dtype in scratch],
        compiler_params=pltpu.CompilerParams(vmem_limit_bytes=48 << 20),
        cost_estimate=cost,
    )(*operands)


SENDS = [(HALO, CH, COLS), (HALO, CH, COLS), (ROWS // 4, CH, COLS), (HALO // 4, CH, COLS), (HALO // 4, CH, COLS)]
TILE = (ROWS, CH, COLS)


def swap_halos(sends, row_count):
    both = [(r, c) for r in range(row_count) for c in range(2)]

    def swap(x, partner):
        perm = [(2 * r + c, 2 * partner(r, c)[0] + partner(r, c)[1]) for r, c in both if 0 <= partner(r, c)[0] < row_count]
        return lax.ppermute(x, ("row", "col"), perm)

    a, b, c, d, e = sends
    across = lambda r: r - 1 if r % 2 == 0 else r + 1
    got_e = swap(e, lambda r, c: (across(r), 1 - c))
    got_b = swap(b, lambda r, c: (across(r), c))
    got_c = swap(c, lambda r, c: (r, 1 - c))
    got_d = swap(d, lambda r, c: (r ^ 1, 1 - c))
    got_a = swap(a, lambda r, c: (r ^ 1, c))
    return got_a, got_b, got_c, got_d, got_e


def swap_mirror(blocks, row_count):
    out = []
    for k, x in enumerate(blocks):
        perm = [(2 * r + c, 2 * (4 * c + ((r % 4) ^ k)) + r // 4) for r in range(row_count) for c in range(2)]
        out.append(lax.ppermute(x, ("row", "col"), perm))
    return out


def on_tile(row_count, maps, weights, biases, dilations):
    half = weights.transpose(0, 2, 3, 1, 4).reshape(LAYERS, 3 * CH, 3 * CH) * jnp.asarray(0.5, BF16)
    bias = jnp.pad((biases * jnp.asarray(0.5, BF16))[:, :, None], ((0, 0), (CH, CH), (0, KDIM - 3 * CH - 1)))
    matrices = jnp.concatenate([half, bias], axis=2)

    tile, *sends = kernel_call(pack_kernel, [TILE] + SENDS, [((CH * ROWS, COLS), F32)], [maps])
    halos = swap_halos(sends, row_count)
    work = [((FULL, CH, 2 * COLS), BF16)] * 2 + [((CH * ROWS, COLS), F32)]
    tile, *blocks = kernel_call(
        functools.partial(first_kernel, row_count),
        [TILE] + [(ROWS, 16, COLS)] * 4,
        work + [((COLS * 16, COLS), F32)],
        [dilations, matrices[:HALF], tile, *halos],
        smem=1,
    )
    blocks = swap_mirror(blocks, row_count)
    tile, *sends = kernel_call(
        mirror_kernel, [TILE] + SENDS, [((4, ROWS, 16, COLS), BF16)], [tile, *blocks]
    )
    halos = swap_halos(sends, row_count)
    (out,) = kernel_call(
        functools.partial(second_kernel, row_count),
        [(CH, ROWS, COLS)],
        work,
        [dilations, matrices[HALF:], tile, *halos],
        smem=1,
    )
    return out


def solution(mesh):
    def step(maps, weights, biases, dilations):
        sizes = mesh.shape
        tiled = (
            sizes["ch"] == 1
            and sizes["col"] == 2
            and sizes["row"] == 8
            and maps.shape == (CH, ROWS * sizes["row"] * sizes["grp"], COLS * 2)
        )
        body = functools.partial(on_tile, sizes["row"]) if tiled else on_device
        return jax.shard_map(
            body,
            mesh=mesh,
            in_specs=(
                P("ch", ("grp", "row"), "col"),
                P(None, None, None, "ch", None),
                P(None, "ch"),
                P(),
            ),
            out_specs=P("ch", ("grp", "row"), "col"),
            check_vma=False,
        )(maps, weights, biases, dilations)

    return step
```

profile of v0, /device:TPU:1, one launch (start us, length us, event | category | flops | bytes accessed | tf_op | source)
XLA Modules:
  0.0 80.5 jit_solution(9003874890685288219)
XLA Ops:
  0.0 1.0 %copy-done = bf16[64,32,128]{2,1,0:T(8,128)(2,1)S(1)} copy-done((bf16[64,32,128]{2,1,0:T(8,128)(2,1)S(1)}, bf16[64,32,128]{2,1,0:T(8,128)(2,1)}, u32[]{:S(2)}) %copy-start) | copy-done | bytes 524312
  1.0 1.2 %shard_map.46 = (bf16[32,64,128]{2,1,0:T(8,128)(2,1)S(1)}, bf16[24,64,128]{2,1,0:T(8,128)(2,1)S(1)}, bf16[24,64,128]{2,1,0:T(8,128)(2,1)S(1)}, bf16[8,64,128]{2,...) custom-call(bf16[64,32,128]{2,1,0:T(8,128)(2,1)S(1)} %copy-done), custom_call_target="tpu_custom_call" | custom-call | tf_op jit(solution)/shard_map/pallas_call | solution.py:282
  2.3 2.6 %collective-permute-start.3 = (bf16[6,64,128]{2,1,0:T(8,128)(2,1)S(1)}, bf16[6,64,128]{2,1,0:T(8,128)(2,1)S(1)}, u32[]{:S(2)}, u32[]{:S(2)}) collective-permute-start(bf16[6,64,128]{2,1,0:T(8,128)(2,1)S(1)} %get-tuple-element.26), channel_id=1, source_target_pairs={{0,3},{1,2},{2,1},{3,0},{4,7},{5,6},{6,5},{7,4},{8,11},{9,10},{10,... | collective-permute-start | bytes 294920 | tf_op jit(solution)/shard_map/ppermute | solution.py:302
  4.8 3.0 %collective-permute-start.4 = (bf16[6,64,128]{2,1,0:T(8,128)(2,1)S(1)}, bf16[6,64,128]{2,1,0:T(8,128)(2,1)S(1)}, u32[]{:S(2)}, u32[]{:S(2)}) collective-permute-start(bf16[6,64,128]{2,1,0:T(8,128)(2,1)S(1)} %get-tuple-element.27), channel_id=1, source_target_pairs={{2,5},{3,4},{4,3},{5,2},{6,9},{7,8},{8,7},{9,6},{10,13},{11,12},{1... | collective-permute-start | bytes 294920 | tf_op jit(solution)/shard_map/ppermute | solution.py:302
  7.8 1.3 %collective-permute-start.2 = (bf16[8,64,128]{2,1,0:T(8,128)(2,1)S(1)}, bf16[8,64,128]{2,1,0:T(8,128)(2,1)S(1)}, u32[]{:S(2)}, u32[]{:S(2)}) collective-permute-start(bf16[8,64,128]{2,1,0:T(8,128)(2,1)S(1)} %get-tuple-element.25), channel_id=1, source_target_pairs={{0,1},{1,0},{2,3},{3,2},{4,5},{5,4},{6,7},{7,6},{8,9},{9,8},{10,11... | collective-permute-start | bytes 393224 | tf_op jit(solution)/shard_map/ppermute | solution.py:302
  9.1 0.0 collective-permute-start
  9.1 3.6 %collective-permute-start.1 = (bf16[24,64,128]{2,1,0:T(8,128)(2,1)S(1)}, bf16[24,64,128]{2,1,0:T(8,128)(2,1)S(1)}, u32[]{:S(2)}, u32[]{:S(2)}) collective-permute-start(bf16[24,64,128]{2,1,0:T(8,128)(2,1)S(1)} %get-tuple-element.24), channel_id=1, source_target_pairs={{2,4},{3,5},{4,2},{5,3},{6,8},{7,9},{8,6},{9,7},{10,12},{11,13},{1... | collective-permute-start | bytes 1179656 | tf_op jit(solution)/shard_map/ppermute | solution.py:302
  12.7 2.2 %multiply_bitcast_fusion = bf16[6,3,64,3,64]{4,2,1,3,0:T(8,128)(2,1)} fusion(bf16[6,3,3,64,64]{4,3,2,1,0:T(8,128)(2,1)} %param.5), kind=kLoop, calls=%fused_computation.2 | loop fusion | flops 221184 | bytes 884736 | tf_op jit(solution)/shard_map/mul | solution.py:323
  14.9 0.2 copy.7
  15.0 3.0 %copy.6 = bf16[6,3,64,3,64]{4,3,2,1,0:T(4,128)(2,1)} copy(bf16[6,3,64,3,64]{4,2,1,3,0:T(8,128)(2,1)} %multiply_bitcast_fusion) | data formatting | bytes 884736 | tf_op jit(solution)/shard_map/mul | solution.py:323
  18.0 3.4 %mul.21 = bf16[6,192,192]{2,1,0:T(8,128)(2,1)} reshape(bf16[6,3,64,3,64]{4,3,2,1,0:T(4,128)(2,1)} %copy.6) | data formatting | bytes 884736 | tf_op jit(solution)/shard_map/mul | solution.py:323
  21.4 1.2 %fusion.1 = bf16[6,192,208]{2,1,0:T(8,128)(2,1)S(1)} fusion(bf16[6,64,1]{2,1,0:T(8,128)(2,1)S(1)} %copy.7, bf16[6,192,192]{2,1,0:T(8,128)(2,1)} %mul.21), kind=kLoop, calls=%fused_computation.3 | loop fusion | flops 1437696 | bytes 922368 | tf_op jit(solution)/shard_map/concatenate | solution.py:325
  22.6 0.0 collective-permute-done.3.d_ref
  22.7 0.0 collective-permute-done.2.c_ref
  22.7 0.0 collective-permute-done.a_ref
  22.7 9.0 %shard_map.47 = (bf16[32,64,128]{2,1,0:T(8,128)(2,1)S(1)}, bf16[32,16,128]{2,1,0:T(8,128)(2,1)S(1)}, bf16[32,16,128]{2,1,0:T(8,128)(2,1)S(1)}, bf16[32,16,128]{2,1,0:T(8,128)(2,1)S(1)}, bf16[32,16,128]{2,1,0:T(8,128)(2,1)S(1)}) custom-call(s32[6]{0:T(128)S(1)} %copy-done.1, bf16[3,192,208]{2,1,0:T(8,128)(2,1)S(1)} %get-tuple-element.39.w_ref, ...), custom_call_target="tpu_custom_call" | custom-call | tf_op jit(solution)/shard_map/pallas_call | solution.py:282
  31.7 0.7 collective-permute-start.5
  32.4 0.1 collective-permute-start.6
  32.5 1.4 %collective-permute-start.7 = (bf16[32,16,128]{2,1,0:T(8,128)(2,1)S(1)}, bf16[32,16,128]{2,1,0:T(8,128)(2,1)S(1)}, u32[]{:S(2)}, u32[]{:S(2)}) collective-permute-start(bf16[32,16,128]{2,1,0:T(8,128)(2,1)S(1)} %get-tuple-element.31), channel_id=1, source_target_pairs={{0,4},{1,12},{2,6},{3,14},{4,0},{5,8},{6,2},{7,10},{8,5},{9,13},{1... | collective-permute-start | bytes 393224 | tf_op jit(solution)/shard_map/ppermute | solution.py:318
  33.8 0.8 collective-permute-start.8
  34.6 0.0 collective-permute-done.5.m0
  34.6 0.0 collective-permute-done.6.m1
  34.6 3.9 %collective-permute-done.7.m2 = bf16[32,16,128]{2,1,0:T(8,128)(2,1)S(1)} collective-permute-done((bf16[32,16,128]{2,1,0:T(8,128)(2,1)S(1)}, bf16[32,16,128]{2,1,0:T(8,128)(2,1)S(1)}, u32[]{:S(2)}, u32[]{:S(2)}) %collective-permute-start.7) | collective-permute-done | bytes 131104 | tf_op jit(solution)/shard_map/ppermute | solution.py:318
  38.5 3.4 %collective-permute-done.8.m3 = bf16[32,16,128]{2,1,0:T(8,128)(2,1)S(1)} collective-permute-done((bf16[32,16,128]{2,1,0:T(8,128)(2,1)S(1)}, bf16[32,16,128]{2,1,0:T(8,128)(2,1)S(1)}, u32[]{:S(2)}, u32[]{:S(2)}) %collective-permute-start.8) | collective-permute-done | bytes 131104 | tf_op jit(solution)/shard_map/ppermute | solution.py:318
  41.9 0.9 %shard_map.48 = (bf16[32,64,128]{2,1,0:T(8,128)(2,1)S(1)}, bf16[24,64,128]{2,1,0:T(8,128)(2,1)S(1)}, bf16[24,64,128]{2,1,0:T(8,128)(2,1)S(1)}, bf16[8,64,128]{2,...) custom-call(bf16[32,64,128]{2,1,0:T(8,128)(2,1)S(1)} %get-tuple-element.28.x_ref, ...), custom_call_target="tpu_custom_call" | custom-call | tf_op jit(solution)/shard_map/pallas_call | solution.py:282
  42.8 0.1 collective-permute-start.9
  42.9 2.2 %collective-permute-start.10 = (bf16[24,64,128]{2,1,0:T(8,128)(2,1)S(1)}, bf16[24,64,128]{2,1,0:T(8,128)(2,1)S(1)}, u32[]{:S(2)}, u32[]{:S(2)}) collective-permute-start(bf16[24,64,128]{2,1,0:T(8,128)(2,1)S(1)} %get-tuple-element.35), channel_id=1, source_target_pairs={{2,4},{3,5},{4,2},{5,3},{6,8},{7,9},{8,6},{9,7},{10,12},{11,13},{1... | collective-permute-start | bytes 1179656 | tf_op jit(solution)/shard_map/ppermute | solution.py:302
  45.1 18.4 %collective-permute-start.11 = (bf16[8,64,128]{2,1,0:T(8,128)(2,1)S(1)}, bf16[8,64,128]{2,1,0:T(8,128)(2,1)S(1)}, u32[]{:S(2)}, u32[]{:S(2)}) collective-permute-start(bf16[8,64,128]{2,1,0:T(8,128)(2,1)S(1)} %get-tuple-element.36), channel_id=1, source_target_pairs={{0,1},{1,0},{2,3},{3,2},{4,5},{5,4},{6,7},{7,6},{8,9},{9,8},{10,11... | collective-permute-start | bytes 393224 | tf_op jit(solution)/shard_map/ppermute | solution.py:302
  63.5 4.0 %collective-permute-start.13 = (bf16[6,64,128]{2,1,0:T(8,128)(2,1)S(1)}, bf16[6,64,128]{2,1,0:T(8,128)(2,1)S(1)}, u32[]{:S(2)}, u32[]{:S(2)}) collective-permute-start(bf16[6,64,128]{2,1,0:T(8,128)(2,1)S(1)} %get-tuple-element.38), channel_id=1, source_target_pairs={{2,5},{3,4},{4,3},{5,2},{6,9},{7,8},{8,7},{9,6},{10,13},{11,12},{1... | collective-permute-start | bytes 294920 | tf_op jit(solution)/shard_map/ppermute | solution.py:302
  67.5 0.4 collective-permute-done.12.d_ref
  67.9 2.4 %collective-permute-done.13.e_ref = bf16[6,64,128]{2,1,0:T(8,128)(2,1)S(1)} collective-permute-done((bf16[6,64,128]{2,1,0:T(8,128)(2,1)S(1)}, bf16[6,64,128]{2,1,0:T(8,128)(2,1)S(1)}, u32[]{:S(2)}, u32[]{:S(2)}) %collective-permute-start.13) | collective-permute-done | bytes 98336 | tf_op jit(solution)/shard_map/ppermute | solution.py:302
  70.3 10.2 %shard_map.49 = bf16[64,32,128]{2,1,0:T(8,128)(2,1)} custom-call(s32[6]{0:T(128)S(1)} %copy-done.1, bf16[3,192,208]{2,1,0:T(8,128)(2,1)S(1)} %get-tuple-element.40.w_ref, bf16[32,64,128]{2,1,0:T(8,128)(2,1)S(1)} %get-tuple-element.33.xt_ref, bf16[24,64,128]{2,1,0:T(8,128)(2,1)S(1)} %collective-permute-done.9.a_ref, ...), custom_call_target="tpu_custom_call" | custom-call | tf_op jit(solution)/shard_map/pallas_call | solution.py:282
  (13 shorter events, 0.1 us)
Async XLA Ops:
  0.0 1.0 %copy-start = (bf16[64,32,128]{2,1,0:T(8,128)(2,1)S(1)}, bf16[64,32,128]{2,1,0:T(8,128)(2,1)}, u32[]{:S(2)}) copy-start(bf16[64,32,128]{2,1,0:T(8,128)(2,1)} %x_ref.1) | copy-start | bytes 1572868
  1.0 13.8 %copy-start.2 = (bf16[6,64]{1,0:T(8,128)(2,1)S(1)}, bf16[6,64]{1,0:T(8,128)(2,1)}, u32[]{:S(2)}) copy-start(bf16[6,64]{1,0:T(8,128)(2,1)} %param.6) | copy-start | bytes 2308
  2.3 20.4 %collective-permute-start.3 = (bf16[6,64,128]{2,1,0:T(8,128)(2,1)S(1)}, bf16[6,64,128]{2,1,0:T(8,128)(2,1)S(1)}, u32[]{:S(2)}, u32[]{:S(2)}) collective-permute-start(bf16[6,64,128]{2,1,0:T(8,128)(2,1)S(1)} %get-tuple-element.26), channel_id=1, source_target_pairs={{0,3},{1,2},{2,1},{3,0},{4,7},{5,6},{6,5},{7,4},{8,11},{9,10},{10,... | collective-permute-start | bytes 294920 | tf_op jit(solution)/shard_map/ppermute | solution.py:302
  4.8 17.8 %collective-permute-start.4 = (bf16[6,64,128]{2,1,0:T(8,128)(2,1)S(1)}, bf16[6,64,128]{2,1,0:T(8,128)(2,1)S(1)}, u32[]{:S(2)}, u32[]{:S(2)}) collective-permute-start(bf16[6,64,128]{2,1,0:T(8,128)(2,1)S(1)} %get-tuple-element.27), channel_id=1, source_target_pairs={{2,5},{3,4},{4,3},{5,2},{6,9},{7,8},{8,7},{9,6},{10,13},{11,12},{1... | collective-permute-start | bytes 294920 | tf_op jit(solution)/shard_map/ppermute | solution.py:302
  7.8 14.8 %collective-permute-start.2 = (bf16[8,64,128]{2,1,0:T(8,128)(2,1)S(1)}, bf16[8,64,128]{2,1,0:T(8,128)(2,1)S(1)}, u32[]{:S(2)}, u32[]{:S(2)}) collective-permute-start(bf16[8,64,128]{2,1,0:T(8,128)(2,1)S(1)} %get-tuple-element.25), channel_id=1, source_target_pairs={{0,1},{1,0},{2,3},{3,2},{4,5},{5,4},{6,7},{7,6},{8,9},{9,8},{10,11... | collective-permute-start | bytes 393224 | tf_op jit(solution)/shard_map/ppermute | solution.py:302
  9.1 13.6 %collective-permute-start = (bf16[24,64,128]{2,1,0:T(8,128)(2,1)S(1)}, bf16[24,64,128]{2,1,0:T(8,128)(2,1)S(1)}, u32[]{:S(2)}, u32[]{:S(2)}) collective-permute-start(bf16[24,64,128]{2,1,0:T(8,128)(2,1)S(1)} %get-tuple-element.23), channel_id=1, source_target_pairs={{0,2},{1,3},{2,0},{3,1},{4,6},{5,7},{6,4},{7,5},{8,10},{9,11},{10,... | collective-permute-start | bytes 1179656 | tf_op jit(solution)/shard_map/ppermute | solution.py:302
  9.1 13.6 %collective-permute-start.1 = (bf16[24,64,128]{2,1,0:T(8,128)(2,1)S(1)}, bf16[24,64,128]{2,1,0:T(8,128)(2,1)S(1)}, u32[]{:S(2)}, u32[]{:S(2)}) collective-permute-start(bf16[24,64,128]{2,1,0:T(8,128)(2,1)S(1)} %get-tuple-element.24), channel_id=1, source_target_pairs={{2,4},{3,5},{4,2},{5,3},{6,8},{7,9},{8,6},{9,7},{10,12},{11,13},{1... | collective-permute-start | bytes 1179656 | tf_op jit(solution)/shard_map/ppermute | solution.py:302
  21.4 1.3 %copy-start.1 = (s32[6]{0:T(128)S(1)}, s32[6]{0:T(128)}, u32[]{:S(2)}) copy-start(s32[6]{0:T(128)} %dil_ref.3) | copy-start | bytes 76
  31.7 2.9 %collective-permute-start.5 = (bf16[32,16,128]{2,1,0:T(8,128)(2,1)S(1)}, bf16[32,16,128]{2,1,0:T(8,128)(2,1)S(1)}, u32[]{:S(2)}, u32[]{:S(2)}) collective-permute-start(bf16[32,16,128]{2,1,0:T(8,128)(2,1)S(1)} %get-tuple-element.29), channel_id=1, source_target_pairs={{0,0},{1,8},{2,2},{3,10},{4,4},{5,12},{6,6},{7,14},{8,1},{9,9},{10... | collective-permute-start | bytes 393224 | tf_op jit(solution)/shard_map/ppermute | solution.py:318
  32.4 2.2 %collective-permute-start.6 = (bf16[32,16,128]{2,1,0:T(8,128)(2,1)S(1)}, bf16[32,16,128]{2,1,0:T(8,128)(2,1)S(1)}, u32[]{:S(2)}, u32[]{:S(2)}) collective-permute-start(bf16[32,16,128]{2,1,0:T(8,128)(2,1)S(1)} %get-tuple-element.30), channel_id=1, source_target_pairs={{0,2},{1,10},{2,0},{3,8},{4,6},{5,14},{6,4},{7,12},{8,3},{9,11},{1... | collective-permute-start | bytes 393224 | tf_op jit(solution)/shard_map/ppermute | solution.py:318
  32.5 6.0 %collective-permute-start.7 = (bf16[32,16,128]{2,1,0:T(8,128)(2,1)S(1)}, bf16[32,16,128]{2,1,0:T(8,128)(2,1)S(1)}, u32[]{:S(2)}, u32[]{:S(2)}) collective-permute-start(bf16[32,16,128]{2,1,0:T(8,128)(2,1)S(1)} %get-tuple-element.31), channel_id=1, source_target_pairs={{0,4},{1,12},{2,6},{3,14},{4,0},{5,8},{6,2},{7,10},{8,5},{9,13},{1... | collective-permute-start | bytes 393224 | tf_op jit(solution)/shard_map/ppermute | solution.py:318
  33.8 8.1 %collective-permute-start.8 = (bf16[32,16,128]{2,1,0:T(8,128)(2,1)S(1)}, bf16[32,16,128]{2,1,0:T(8,128)(2,1)S(1)}, u32[]{:S(2)}, u32[]{:S(2)}) collective-permute-start(bf16[32,16,128]{2,1,0:T(8,128)(2,1)S(1)} %get-tuple-element.32), channel_id=1, source_target_pairs={{0,6},{1,14},{2,4},{3,12},{4,2},{5,10},{6,0},{7,8},{8,7},{9,15},{1... | collective-permute-start | bytes 393224 | tf_op jit(solution)/shard_map/ppermute | solution.py:318
  42.8 27.5 %collective-permute-start.9 = (bf16[24,64,128]{2,1,0:T(8,128)(2,1)S(1)}, bf16[24,64,128]{2,1,0:T(8,128)(2,1)S(1)}, u32[]{:S(2)}, u32[]{:S(2)}) collective-permute-start(bf16[24,64,128]{2,1,0:T(8,128)(2,1)S(1)} %get-tuple-element.34), channel_id=1, source_target_pairs={{0,2},{1,3},{2,0},{3,1},{4,6},{5,7},{6,4},{7,5},{8,10},{9,11},{10,... | collective-permute-start | bytes 1179656 | tf_op jit(solution)/shard_map/ppermute | solution.py:302
  42.9 27.4 %collective-permute-start.10 = (bf16[24,64,128]{2,1,0:T(8,128)(2,1)S(1)}, bf16[24,64,128]{2,1,0:T(8,128)(2,1)S(1)}, u32[]{:S(2)}, u32[]{:S(2)}) collective-permute-start(bf16[24,64,128]{2,1,0:T(8,128)(2,1)S(1)} %get-tuple-element.35), channel_id=1, source_target_pairs={{2,4},{3,5},{4,2},{5,3},{6,8},{7,9},{8,6},{9,7},{10,12},{11,13},{1... | collective-permute-start | bytes 1179656 | tf_op jit(solution)/shard_map/ppermute | solution.py:302
  45.1 25.2 %collective-permute-start.11 = (bf16[8,64,128]{2,1,0:T(8,128)(2,1)S(1)}, bf16[8,64,128]{2,1,0:T(8,128)(2,1)S(1)}, u32[]{:S(2)}, u32[]{:S(2)}) collective-permute-start(bf16[8,64,128]{2,1,0:T(8,128)(2,1)S(1)} %get-tuple-element.36), channel_id=1, source_target_pairs={{0,1},{1,0},{2,3},{3,2},{4,5},{5,4},{6,7},{7,6},{8,9},{9,8},{10,11... | collective-permute-start | bytes 393224 | tf_op jit(solution)/shard_map/ppermute | solution.py:302
  63.5 4.5 %collective-permute-start.12 = (bf16[6,64,128]{2,1,0:T(8,128)(2,1)S(1)}, bf16[6,64,128]{2,1,0:T(8,128)(2,1)S(1)}, u32[]{:S(2)}, u32[]{:S(2)}) collective-permute-start(bf16[6,64,128]{2,1,0:T(8,128)(2,1)S(1)} %get-tuple-element.37), channel_id=1, source_target_pairs={{0,3},{1,2},{2,1},{3,0},{4,7},{5,6},{6,5},{7,4},{8,11},{9,10},{10,... | collective-permute-start | bytes 294920 | tf_op jit(solution)/shard_map/ppermute | solution.py:302
  63.5 6.8 %collective-permute-start.13 = (bf16[6,64,128]{2,1,0:T(8,128)(2,1)S(1)}, bf16[6,64,128]{2,1,0:T(8,128)(2,1)S(1)}, u32[]{:S(2)}, u32[]{:S(2)}) collective-permute-start(bf16[6,64,128]{2,1,0:T(8,128)(2,1)S(1)} %get-tuple-element.38), channel_id=1, source_target_pairs={{2,5},{3,4},{4,3},{5,2},{6,9},{7,8},{8,7},{9,6},{10,13},{11,12},{1... | collective-permute-start | bytes 294920 | tf_op jit(solution)/shard_map/ppermute | solution.py:302
where the time goes:
time: 81.4 us; the launch traced here: 80.5 us
  starting transfers between devices  38 us (47%)
  Pallas kernels  21.3 us (26%)
  waiting for transfers between devices  10.1 us (12%)
  local copies, waits for them, and re-layouts  7.58 us (9%)
  other arithmetic  3.4 us (4%)
    ppermute x10, starting transfers between devices, swap(): return lax.ppermute(x, ('row', 'col'), perm)  35.1 us
    pallas_call x4, Pallas kernels, kernel_call(): pl.pallas_call(body, out_shape=[jax.ShapeDtypeStruct(shape, BF16) for sha...  21.3 us
    ppermute x4, waiting for transfers between devices, swap_mirror(): out.append(lax.ppermute(x, ('row', 'col'), perm))  7.32 us
    mul x2, local copies, waits for them, and re-layouts, on_tile(): weights.transpose(0, 2, 3, 1, 4).reshape(LAYERS, 3 * CH, 3 * CH)  6.34 us
    ppermute x4, starting transfers between devices, swap_mirror(): out.append(lax.ppermute(x, ('row', 'col'), perm))  2.87 us
    ppermute x10, waiting for transfers between devices, swap(): return lax.ppermute(x, ('row', 'col'), perm)  2.8 us
    mul x1, other arithmetic, on_tile(): weights.transpose(0, 2, 3, 1, 4).reshape(LAYERS, 3 * CH, 3 * CH)  2.17 us
  transfers between devices with their start and end apart: 14, of which 4 were waited for; matrix products, arithmetic and copies ran while one was open for 12% of the time, Pallas kernels for 0%

commit v1 on v0

--- a/solution.py
+++ b/solution.py
@@ -103,6 +103,7 @@
 COLS = 128
 HALF = LAYERS // 2
 HALO = HALF * DMAX
+EDGE_SLOTS = COLS // HALO
 SLOT = 32
 FULL = ROWS + 2 * HALO
 KDIM = 3 * CH + 16
@@ -116,13 +117,20 @@
     return r, c, lax.rem(r, 2)
 
 
-def edge_pack(row_of, out_ref, c, start, groups):
+def edge_groups(rows):
+    return -(-rows // EDGE_SLOTS)
+
+
+def edge_pack(row_of, out_ref, c, start, rows):
     lane = lax.broadcasted_iota(jnp.int32, (CH, COLS), 1)
+    groups = edge_groups(rows)
     for t in range(groups):
         acc = None
-        for q in range(4):
-            piece = pltpu.roll(row_of(start + t + groups * q), lax.rem(SLOT * (q + 1 - c), COLS), 1)
-            acc = piece if acc is None else jnp.where(lane >= SLOT * q, piece, acc)
+        for q in range(EDGE_SLOTS):
+            i = t + groups * q
+            if i < rows:
+                piece = pltpu.roll(row_of(start + i), lax.rem(HALO * (q + 1 - c) + c * COLS, COLS), 1)
+                acc = piece if acc is None else jnp.where(lane >= HALO * q, piece, acc)
         out_ref[t] = acc.astype(BF16)
 
 
@@ -136,9 +144,9 @@
     def row_of(i):
         return read(i).astype(F32)
 
-    edge_pack(row_of, c_ref, c, 0, ROWS // 4)
-    edge_pack(row_of, d_ref, c, off_a, HALO // 4)
-    edge_pack(row_of, e_ref, c, off_b, HALO // 4)
+    edge_pack(row_of, c_ref, c, 0, ROWS)
+    edge_pack(row_of, d_ref, c, off_a, HALO)
+    edge_pack(row_of, e_ref, c, off_b, HALO)
 
 
 def pack_kernel(x_ref, xt_ref, a_ref, b_ref, c_ref, d_ref, e_ref, flat):
@@ -151,8 +159,8 @@
 
 def assemble(xa, xt_ref, a_ref, b_ref, c_ref, d_ref, e_ref, c, core):
     lane = lax.broadcasted_iota(jnp.int32, (CH, COLS), 1)
-    first = c * (COLS - SLOT)
-    mask = (lane >= first) & (lane < first + SLOT)
+    first = c * (COLS - HALO)
+    mask = (lane >= first) & (lane < first + HALO)
     at_a = (FULL - HALO) * (1 - core)
     at_b = (FULL - HALO) * core
     for i in range(ROWS):
@@ -160,12 +168,15 @@
     for i in range(HALO):
         xa[at_a + i, :, 0:COLS] = a_ref[i]
         xa[at_b + i, :, 0:COLS] = b_ref[i]
-    for ref, start, groups in ((c_ref, HALO, ROWS // 4), (d_ref, at_a, HALO // 4), (e_ref, at_b, HALO // 4)):
+    for ref, start, rows in ((c_ref, HALO, ROWS), (d_ref, at_a, HALO), (e_ref, at_b, HALO)):
+        groups = edge_groups(rows)
         for t in range(groups):
             packed = ref[t].astype(F32)
-            for q in range(4):
-                piece = pltpu.roll(packed, lax.rem(COLS + first - SLOT * q, COLS), 1)
-                xa[start + t + groups * q, :, COLS:] = jnp.where(mask, piece, 0.0).astype(BF16)
+            for q in range(EDGE_SLOTS):
+                i = t + groups * q
+                if i < rows:
+                    piece = pltpu.roll(packed, lax.rem(COLS + first - HALO * q, COLS), 1)
+                    xa[start + i, :, COLS:] = jnp.where(mask, piece, 0.0).astype(BF16)
     return mask
 
 
@@ -192,7 +203,7 @@
 
         def row(h, src=src, dst=dst, s=s, layer=layer, fl=from_left, fr=from_right, final=final):
             taps = jnp.concatenate([src[h - s], src[h], src[h + s], ones], axis=0)
-            y = jnp.dot(w_ref[layer], taps, preferred_element_type=F32)
+            y = jnp.dot(w_ref[base + layer], taps, preferred_element_type=F32)
             left = [pltpu.roll(y[0:CH, k * COLS : (k + 1) * COLS], s, 1) for k in range(2)]
             right = [pltpu.roll(y[2 * CH :, k * COLS : (k + 1) * COLS], COLS - s, 1) for k in range(2)]
             for k in range(1 if final else 2):
@@ -220,6 +231,21 @@
         src, dst = dst, src
 
 
+def weights_kernel(w_ref, bias_ref, o_ref):
+    row = lax.broadcasted_iota(jnp.int32, (CH, CH), 0)
+    col = lax.broadcasted_iota(jnp.int32, (CH, CH), 1)
+    lane = lax.broadcasted_iota(jnp.int32, (CH, KDIM - 3 * CH), 1)
+    for layer in range(LAYERS):
+        bias = jnp.broadcast_to(bias_ref[layer : layer + 1, :].astype(F32) * 0.5, (CH, CH))
+        column = jnp.sum(jnp.where(row == col, bias, 0.0), axis=1, keepdims=True)
+        extra = jnp.where(lane == 0, column, 0.0).astype(BF16)
+        none = jnp.zeros((CH, KDIM - 3 * CH), BF16)
+        for b in range(3):
+            taps = jnp.concatenate([w_ref[layer, a, b] for a in range(3)], axis=1)
+            o_ref[layer, b * CH : (b + 1) * CH, 0 : 3 * CH] = (taps.astype(F32) * 0.5).astype(BF16)
+            o_ref[layer, b * CH : (b + 1) * CH, 3 * CH :] = extra if b == 1 else none
+
+
 def first_kernel(row_count, dil_ref, w_ref, xt_ref, a_ref, b_ref, c_ref, d_ref, e_ref,
                  x_ref, m0, m1, m2, m3, xa, xb, flat, turned):
     r, c, core = place()
@@ -240,11 +266,16 @@
         ref[...] = turned[pl.ds(start, ROWS * 16), :].reshape(ROWS, 16, COLS).astype(BF16)
 
 
-def mirror_kernel(x_ref, m0, m1, m2, m3, xt_ref, a_ref, b_ref, c_ref, d_ref, e_ref, got):
+def mirror_kernel(x_ref, own, m0, m1, m2, m3, xt_ref, a_ref, b_ref, c_ref, d_ref, e_ref, got):
     r, c, core = place()
     rr = lax.rem(r, 4)
     for k, ref in enumerate((m0, m1, m2, m3)):
         got[jnp.bitwise_xor(rr, k)] = ref[...]
+
+    @pl.when(r // 4 == c)
+    def _():
+        got[rr] = own[...]
+
     slot = lax.broadcasted_iota(jnp.int32, (16, COLS), 1) // SLOT
 
     def by_slot(pieces):
@@ -290,7 +321,9 @@
     )(*operands)
 
 
-SENDS = [(HALO, CH, COLS), (HALO, CH, COLS), (ROWS // 4, CH, COLS), (HALO // 4, CH, COLS), (HALO // 4, CH, COLS)]
+ROW_SENDS = [(HALO, CH, COLS)] * 2
+EDGE_SENDS = [(edge_groups(rows), CH, COLS) for rows in (ROWS, HALO, HALO)]
+SENDS = ROW_SENDS + EDGE_SENDS
 TILE = (ROWS, CH, COLS)
 
 
@@ -312,18 +345,20 @@
 
 
 def swap_mirror(blocks, row_count):
-    out = []
-    for k, x in enumerate(blocks):
-        perm = [(2 * r + c, 2 * (4 * c + ((r % 4) ^ k)) + r // 4) for r in range(row_count) for c in range(2)]
-        out.append(lax.ppermute(x, ("row", "col"), perm))
-    return out
+    both = [(r, c) for r in range(row_count) for c in range(2)]
+    near = [(r, c) for r, c in both if r // 4 == c]
+    far = [(r, c) for r, c in both if r // 4 != c]
+
+    def send(x, sources, target):
+        return lax.ppermute(x, ("row", "col"), [(2 * r + c, 2 * target(r, c)[0] + target(r, c)[1]) for r, c in sources])
+
+    crossed = send(blocks[0], far, lambda r, c: (r, 1 - c))
+    out = [send(blocks[k], both, lambda r, c, k=k: (4 * c + ((r % 4) ^ k), r // 4)) for k in range(1, 4)]
+    return [send(crossed, near, lambda r, c: (r ^ 4, c)), *out]
 
 
 def on_tile(row_count, maps, weights, biases, dilations):
-    half = weights.transpose(0, 2, 3, 1, 4).reshape(LAYERS, 3 * CH, 3 * CH) * jnp.asarray(0.5, BF16)
-    bias = jnp.pad((biases * jnp.asarray(0.5, BF16))[:, :, None], ((0, 0), (CH, CH), (0, KDIM - 3 * CH - 1)))
-    matrices = jnp.concatenate([half, bias], axis=2)
-
+    (matrices,) = kernel_call(weights_kernel, [(LAYERS, 3 * CH, KDIM)], [], [weights, biases])
     tile, *sends = kernel_call(pack_kernel, [TILE] + SENDS, [((CH * ROWS, COLS), F32)], [maps])
     halos = swap_halos(sends, row_count)
     work = [((FULL, CH, 2 * COLS), BF16)] * 2 + [((CH * ROWS, COLS), F32)]
@@ -331,19 +366,19 @@
         functools.partial(first_kernel, row_count),
         [TILE] + [(ROWS, 16, COLS)] * 4,
         work + [((COLS * 16, COLS), F32)],
-        [dilations, matrices[:HALF], tile, *halos],
+        [dilations, matrices, tile, *halos],
         smem=1,
     )
-    blocks = swap_mirror(blocks, row_count)
+    mirrored = swap_mirror(blocks, row_count)
     tile, *sends = kernel_call(
-        mirror_kernel, [TILE] + SENDS, [((4, ROWS, 16, COLS), BF16)], [tile, *blocks]
+        mirror_kernel, [TILE] + SENDS, [((4, ROWS, 16, COLS), BF16)], [tile, blocks[0], *mirrored]
     )
     halos = swap_halos(sends, row_count)
     (out,) = kernel_call(
         functools.partial(second_kernel, row_count),
         [(CH, ROWS, COLS)],
         work,
-        [dilations, matrices[HALF:], tile, *halos],
+        [dilations, matrices, tile, *halos],
         smem=1,
     )
     return out

time: 81.4 us -> 69.4 us (0.85)
  starting transfers between devices: 38 us -> 32.3 us
  local copies, waits for them, and re-layouts: 7.58 us -> 2.48 us
  other arithmetic: 3.4 us -> 0 us
  waiting for transfers between devices: 10.1 us -> 12.6 us
    ppermute x10, starting transfers between devices: 35.1 us -> 23.3 us  [swap(): return lax.ppermute(x, ('row', 'col'), perm)]
    mul x2 -> x0, local copies, waits for them, and re-layouts: 6.34 us -> none  [on_tile(): weights.transpose(0, 2, 3, 1, 4).reshape(LAYERS, 3 * CH, 3 * CH)]
    ppermute x4 -> x5, starting transfers between devices: 2.87 us -> 8.93 us  [send(): lax.ppermute(x, ('row', 'col'), [(2 * r + c, 2 * target(r, c)[0] + target...]
    ppermute x4 -> x5, waiting for transfers between devices: 7.32 us -> 9.55 us  [send(): lax.ppermute(x, ('row', 'col'), [(2 * r + c, 2 * target(r, c)[0] + target...]
    mul x1 -> x0, other arithmetic: 2.17 us -> none  [on_tile(): weights.transpose(0, 2, 3, 1, 4).reshape(LAYERS, 3 * CH, 3 * CH)]
    unnamed x6 -> x8, local copies, waits for them, and re-layouts: 1.05 us -> 2.48 us
    concatenate x1 -> x0, other arithmetic: 1.22 us -> none  [on_tile(): matrices = jnp.concatenate([half, bias], axis=2)]
    pallas_call x4 -> x5, Pallas kernels: 21.3 us -> 20.7 us  [kernel_call(): pl.pallas_call(body, out_shape=[jax.ShapeDtypeStruct(shape, BF16) for sha...]
  transfers between devices with their start and end apart: 14 -> 15, of which waited for: 4 -> 4; matrix products, arithmetic and copies ran while one was open for 12% -> 0% of each run, Pallas kernels for 0% -> 1%
where the time goes in v1:
time: 69.4 us; the launch traced here: 68.2 us
  starting transfers between devices  32.3 us (47%)
  Pallas kernels  20.7 us (30%)
  waiting for transfers between devices  12.6 us (18%)
  local copies, waits for them, and re-layouts  2.48 us (4%)
    ppermute x10, starting transfers between devices, swap(): return lax.ppermute(x, ('row', 'col'), perm)  23.3 us
    pallas_call x5, Pallas kernels, kernel_call(): pl.pallas_call(body, out_shape=[jax.ShapeDtypeStruct(shape, BF16) for sha...  20.7 us
    ppermute x5, waiting for transfers between devices, send(): lax.ppermute(x, ('row', 'col'), [(2 * r + c, 2 * target(r, c)[0] + target...  9.55 us
    ppermute x5, starting transfers between devices, send(): lax.ppermute(x, ('row', 'col'), [(2 * r + c, 2 * target(r, c)[0] + target...  8.93 us
    ppermute x10, waiting for transfers between devices, swap(): return lax.ppermute(x, ('row', 'col'), perm)  3.09 us
    unnamed x8, local copies, waits for them, and re-layouts  2.48 us
  transfers between devices with their start and end apart: 15, of which 4 were waited for; matrix products, arithmetic and copies ran while one was open for 0% of the time, Pallas kernels for 1%

profile of v1, /device:TPU:1, one launch (start us, length us, event | category | flops | bytes accessed | tf_op | source)
XLA Modules:
  0.0 68.2 jit_solution(16132448658087017271)
XLA Ops:
  0.0 1.0 %copy-done.1 = bf16[64,32,128]{2,1,0:T(8,128)(2,1)S(1)} copy-done((bf16[64,32,128]{2,1,0:T(8,128)(2,1)S(1)}, bf16[64,32,128]{2,1,0:T(8,128)(2,1)}, u32[]{:S(2)}) %copy-start.1) | copy-done | bytes 524312
  1.0 1.2 %shard_map.47 = (bf16[32,64,128]{2,1,0:T(8,128)(2,1)S(1)}, bf16[24,64,128]{2,1,0:T(8,128)(2,1)S(1)}, bf16[24,64,128]{2,1,0:T(8,128)(2,1)S(1)}, bf16[7,64,128]{2,...) custom-call(bf16[64,32,128]{2,1,0:T(8,128)(2,1)S(1)} %copy-done.1), custom_call_target="tpu_custom_call" | custom-call | tf_op jit(solution)/shard_map/pallas_call | solution.py:313
  2.2 0.1 collective-permute-start
  2.3 4.5 %collective-permute-start.1 = (bf16[24,64,128]{2,1,0:T(8,128)(2,1)S(1)}, bf16[24,64,128]{2,1,0:T(8,128)(2,1)S(1)}, u32[]{:S(2)}, u32[]{:S(2)}) collective-permute-start(bf16[24,64,128]{2,1,0:T(8,128)(2,1)S(1)} %get-tuple-element.24), channel_id=1, source_target_pairs={{2,4},{3,5},{4,2},{5,3},{6,8},{7,9},{8,6},{9,7},{10,12},{11,13},{1... | collective-permute-start | bytes 1179656 | tf_op jit(solution)/shard_map/ppermute | solution.py:335
  6.9 0.0 copy-start.2
  6.9 1.3 %collective-permute-start.2 = (bf16[7,64,128]{2,1,0:T(8,128)(2,1)S(1)}, bf16[7,64,128]{2,1,0:T(8,128)(2,1)S(1)}, u32[]{:S(2)}, u32[]{:S(2)}) collective-permute-start(bf16[7,64,128]{2,1,0:T(8,128)(2,1)S(1)} %get-tuple-element.25), channel_id=1, source_target_pairs={{0,1},{1,0},{2,3},{3,2},{4,5},{5,4},{6,7},{7,6},{8,9},{9,8},{10,11... | collective-permute-start | bytes 344072 | tf_op jit(solution)/shard_map/ppermute | solution.py:335
  8.1 0.0 collective-permute-start.3
  8.2 4.7 %collective-permute-start.4 = (bf16[5,64,128]{2,1,0:T(8,128)(2,1)S(1)}, bf16[5,64,128]{2,1,0:T(8,128)(2,1)S(1)}, u32[]{:S(2)}, u32[]{:S(2)}) collective-permute-start(bf16[5,64,128]{2,1,0:T(8,128)(2,1)S(1)} %get-tuple-element.27), channel_id=1, source_target_pairs={{2,5},{3,4},{4,3},{5,2},{6,9},{7,8},{8,7},{9,6},{10,13},{11,12},{1... | collective-permute-start | bytes 245768 | tf_op jit(solution)/shard_map/ppermute | solution.py:335
  12.8 0.0 copy-start
  12.8 1.2 %copy-done = bf16[6,3,3,64,64]{4,3,2,1,0:T(8,128)(2,1)S(1)} copy-done((bf16[6,3,3,64,64]{4,3,2,1,0:T(8,128)(2,1)S(1)}, bf16[6,3,3,64,64]{4,3,2,1,0:T(8,128)(2,1)}, u32[]{:S(2)}) %copy-start) | copy-done | bytes 442392
  14.0 0.5 shard_map.46.w_ref
  14.5 0.0 copy-start.3
  14.6 0.4 collective-permute-done.4.e_ref
  14.9 0.0 collective-permute-done.1.b_ref
  14.9 0.3 copy-done.3
  15.2 8.9 %shard_map.48 = (bf16[32,64,128]{2,1,0:T(8,128)(2,1)S(1)}, bf16[32,16,128]{2,1,0:T(8,128)(2,1)S(1)}, bf16[32,16,128]{2,1,0:T(8,128)(2,1)S(1)}, bf16[32,16,128]{2,1,0:T(8,128)(2,1)S(1)}, bf16[32,16,128]{2,1,0:T(8,128)(2,1)S(1)}) custom-call(s32[6]{0:T(128)S(1)} %copy-done.3, bf16[6,192,208]{2,1,0:T(8,128)(2,1)S(1)} %shard_map.46.w_ref, ...), custom_call_target="tpu_custom_call" | custom-call | tf_op jit(solution)/shard_map/pallas_call | solution.py:313
  24.1 1.3 %collective-permute-start.5 = (bf16[32,16,128]{2,1,0:T(8,128)(2,1)S(1)}, bf16[32,16,128]{2,1,0:T(8,128)(2,1)S(1)}, u32[]{:S(2)}, u32[]{:S(2)}) collective-permute-start(bf16[32,16,128]{2,1,0:T(8,128)(2,1)S(1)} %get-tuple-element.29.own), channel_id=1, source_target_pairs={{1,0},{3,2},{5,4},{7,6},{8,9},{10,11},{12,13},{14,15},{17,16},{19,... | collective-permute-start | bytes 393224 | tf_op jit(solution)/shard_map/ppermute | solution.py:353
  25.4 0.1 collective-permute-start.7
  25.5 2.3 %collective-permute-start.8 = (bf16[32,16,128]{2,1,0:T(8,128)(2,1)S(1)}, bf16[32,16,128]{2,1,0:T(8,128)(2,1)S(1)}, u32[]{:S(2)}, u32[]{:S(2)}) collective-permute-start(bf16[32,16,128]{2,1,0:T(8,128)(2,1)S(1)} %get-tuple-element.31), channel_id=1, source_target_pairs={{0,4},{1,12},{2,6},{3,14},{4,0},{5,8},{6,2},{7,10},{8,5},{9,13},{1... | collective-permute-start | bytes 393224 | tf_op jit(solution)/shard_map/ppermute | solution.py:353
  27.7 0.0 collective-permute-start.9
  27.8 2.3 %collective-permute-done.5 = bf16[32,16,128]{2,1,0:T(8,128)(2,1)S(1)} collective-permute-done((bf16[32,16,128]{2,1,0:T(8,128)(2,1)S(1)}, bf16[32,16,128]{2,1,0:T(8,128)(2,1)S(1)}, u32[]{:S(2)}, u32[]{:S(2)}) %collective-permute-start.5) | collective-permute-done | bytes 131104 | tf_op jit(solution)/shard_map/ppermute | solution.py:353
  30.1 5.3 %collective-permute-start.6 = (bf16[32,16,128]{2,1,0:T(8,128)(2,1)S(1)}, bf16[32,16,128]{2,1,0:T(8,128)(2,1)S(1)}, u32[]{:S(2)}, u32[]{:S(2)}) collective-permute-start(bf16[32,16,128]{2,1,0:T(8,128)(2,1)S(1)} %collective-permute-done.5), channel_id=1, source_target_pairs={{0,8},{2,10},{4,12},{6,14},{9,1},{11,3},{13,5},{15,7},{16,24},{18,... | collective-permute-start | bytes 393224 | tf_op jit(solution)/shard_map/ppermute | solution.py:353
  35.4 0.0 collective-permute-done.8.m2
  35.4 7.2 %collective-permute-done.9.m3 = bf16[32,16,128]{2,1,0:T(8,128)(2,1)S(1)} collective-permute-done((bf16[32,16,128]{2,1,0:T(8,128)(2,1)S(1)}, bf16[32,16,128]{2,1,0:T(8,128)(2,1)S(1)}, u32[]{:S(2)}, u32[]{:S(2)}) %collective-permute-start.9) | collective-permute-done | bytes 131104 | tf_op jit(solution)/shard_map/ppermute | solution.py:353
  42.6 0.9 %shard_map.49 = (bf16[32,64,128]{2,1,0:T(8,128)(2,1)S(1)}, bf16[24,64,128]{2,1,0:T(8,128)(2,1)S(1)}, bf16[24,64,128]{2,1,0:T(8,128)(2,1)S(1)}, bf16[7,64,128]{2,...) custom-call(bf16[32,64,128]{2,1,0:T(8,128)(2,1)S(1)} %get-tuple-element.28.x_ref, ...), custom_call_target="tpu_custom_call" | custom-call | tf_op jit(solution)/shard_map/pallas_call | solution.py:313
  43.5 0.2 collective-permute-start.10
  43.7 2.1 %collective-permute-start.11 = (bf16[24,64,128]{2,1,0:T(8,128)(2,1)S(1)}, bf16[24,64,128]{2,1,0:T(8,128)(2,1)S(1)}, u32[]{:S(2)}, u32[]{:S(2)}) collective-permute-start(bf16[24,64,128]{2,1,0:T(8,128)(2,1)S(1)} %get-tuple-element.35), channel_id=1, source_target_pairs={{2,4},{3,5},{4,2},{5,3},{6,8},{7,9},{8,6},{9,7},{10,12},{11,13},{1... | collective-permute-start | bytes 1179656 | tf_op jit(solution)/shard_map/ppermute | solution.py:335
  45.8 6.6 %collective-permute-start.12 = (bf16[7,64,128]{2,1,0:T(8,128)(2,1)S(1)}, bf16[7,64,128]{2,1,0:T(8,128)(2,1)S(1)}, u32[]{:S(2)}, u32[]{:S(2)}) collective-permute-start(bf16[7,64,128]{2,1,0:T(8,128)(2,1)S(1)} %get-tuple-element.36), channel_id=1, source_target_pairs={{0,1},{1,0},{2,3},{3,2},{4,5},{5,4},{6,7},{7,6},{8,9},{9,8},{10,11... | collective-permute-start | bytes 344072 | tf_op jit(solution)/shard_map/ppermute | solution.py:335
  52.4 3.9 %collective-permute-start.14 = (bf16[5,64,128]{2,1,0:T(8,128)(2,1)S(1)}, bf16[5,64,128]{2,1,0:T(8,128)(2,1)S(1)}, u32[]{:S(2)}, u32[]{:S(2)}) collective-permute-start(bf16[5,64,128]{2,1,0:T(8,128)(2,1)S(1)} %get-tuple-element.38), channel_id=1, source_target_pairs={{2,5},{3,4},{4,3},{5,2},{6,9},{7,8},{8,7},{9,6},{10,13},{11,12},{1... | collective-permute-start | bytes 245768 | tf_op jit(solution)/shard_map/ppermute | solution.py:335
  56.3 0.0 collective-permute-done.13.d_ref
  56.3 2.7 %collective-permute-done.14.e_ref = bf16[5,64,128]{2,1,0:T(8,128)(2,1)S(1)} collective-permute-done((bf16[5,64,128]{2,1,0:T(8,128)(2,1)S(1)}, bf16[5,64,128]{2,1,0:T(8,128)(2,1)S(1)}, u32[]{:S(2)}, u32[]{:S(2)}) %collective-permute-start.14) | collective-permute-done | bytes 81952 | tf_op jit(solution)/shard_map/ppermute | solution.py:335
  59.0 9.2 %shard_map.50 = bf16[64,32,128]{2,1,0:T(8,128)(2,1)} custom-call(s32[6]{0:T(128)S(1)} %copy-done.3, bf16[6,192,208]{2,1,0:T(8,128)(2,1)S(1)} %shard_map.46.w_ref, bf16[32,64,128]{2,1,0:T(8,128)(2,1)S(1)} %get-tuple-element.33.xt_ref, bf16[24,64,128]{2,1,0:T(8,128)(2,1)S(1)} %collective-permute-done.10.a_ref, ...), custom_call_target="tpu_custom_call" | custom-call | tf_op jit(solution)/shard_map/pallas_call | solution.py:313
  (11 shorter events, 0.0 us)
Async XLA Ops:
  0.0 1.0 %copy-start.1 = (bf16[64,32,128]{2,1,0:T(8,128)(2,1)S(1)}, bf16[64,32,128]{2,1,0:T(8,128)(2,1)}, u32[]{:S(2)}) copy-start(bf16[64,32,128]{2,1,0:T(8,128)(2,1)} %x_ref.1) | copy-start | bytes 1572868
  2.2 12.7 %collective-permute-start = (bf16[24,64,128]{2,1,0:T(8,128)(2,1)S(1)}, bf16[24,64,128]{2,1,0:T(8,128)(2,1)S(1)}, u32[]{:S(2)}, u32[]{:S(2)}) collective-permute-start(bf16[24,64,128]{2,1,0:T(8,128)(2,1)S(1)} %get-tuple-element.23), channel_id=1, source_target_pairs={{0,2},{1,3},{2,0},{3,1},{4,6},{5,7},{6,4},{7,5},{8,10},{9,11},{10,... | collective-permute-start | bytes 1179656 | tf_op jit(solution)/shard_map/ppermute | solution.py:335
  2.3 12.6 %collective-permute-start.1 = (bf16[24,64,128]{2,1,0:T(8,128)(2,1)S(1)}, bf16[24,64,128]{2,1,0:T(8,128)(2,1)S(1)}, u32[]{:S(2)}, u32[]{:S(2)}) collective-permute-start(bf16[24,64,128]{2,1,0:T(8,128)(2,1)S(1)} %get-tuple-element.24), channel_id=1, source_target_pairs={{2,4},{3,5},{4,2},{5,3},{6,8},{7,9},{8,6},{9,7},{10,12},{11,13},{1... | collective-permute-start | bytes 1179656 | tf_op jit(solution)/shard_map/ppermute | solution.py:335
  6.9 6.0 %copy-start.2 = (bf16[6,64]{1,0:T(8,128)(2,1)S(1)}, bf16[6,64]{1,0:T(8,128)(2,1)}, u32[]{:S(2)}) copy-start(bf16[6,64]{1,0:T(8,128)(2,1)} %bias_ref.1) | copy-start | bytes 2308
  6.9 8.1 %collective-permute-start.2 = (bf16[7,64,128]{2,1,0:T(8,128)(2,1)S(1)}, bf16[7,64,128]{2,1,0:T(8,128)(2,1)S(1)}, u32[]{:S(2)}, u32[]{:S(2)}) collective-permute-start(bf16[7,64,128]{2,1,0:T(8,128)(2,1)S(1)} %get-tuple-element.25), channel_id=1, source_target_pairs={{0,1},{1,0},{2,3},{3,2},{4,5},{5,4},{6,7},{7,6},{8,9},{9,8},{10,11... | collective-permute-start | bytes 344072 | tf_op jit(solution)/shard_map/ppermute | solution.py:335
  8.1 6.4 %collective-permute-start.3 = (bf16[5,64,128]{2,1,0:T(8,128)(2,1)S(1)}, bf16[5,64,128]{2,1,0:T(8,128)(2,1)S(1)}, u32[]{:S(2)}, u32[]{:S(2)}) collective-permute-start(bf16[5,64,128]{2,1,0:T(8,128)(2,1)S(1)} %get-tuple-element.26), channel_id=1, source_target_pairs={{0,3},{1,2},{2,1},{3,0},{4,7},{5,6},{6,5},{7,4},{8,11},{9,10},{10,... | collective-permute-start | bytes 245768 | tf_op jit(solution)/shard_map/ppermute | solution.py:335
  8.2 6.8 %collective-permute-start.4 = (bf16[5,64,128]{2,1,0:T(8,128)(2,1)S(1)}, bf16[5,64,128]{2,1,0:T(8,128)(2,1)S(1)}, u32[]{:S(2)}, u32[]{:S(2)}) collective-permute-start(bf16[5,64,128]{2,1,0:T(8,128)(2,1)S(1)} %get-tuple-element.27), channel_id=1, source_target_pairs={{2,5},{3,4},{4,3},{5,2},{6,9},{7,8},{8,7},{9,6},{10,13},{11,12},{1... | collective-permute-start | bytes 245768 | tf_op jit(solution)/shard_map/ppermute | solution.py:335
  12.8 1.2 %copy-start = (bf16[6,3,3,64,64]{4,3,2,1,0:T(8,128)(2,1)S(1)}, bf16[6,3,3,64,64]{4,3,2,1,0:T(8,128)(2,1)}, u32[]{:S(2)}) copy-start(bf16[6,3,3,64,64]{4,3,2,1,0:T(8,128)(2,1)} %w_ref.1) | copy-start | bytes 1327108
  14.5 0.7 copy-start.3
  24.1 6.0 %collective-permute-start.5 = (bf16[32,16,128]{2,1,0:T(8,128)(2,1)S(1)}, bf16[32,16,128]{2,1,0:T(8,128)(2,1)S(1)}, u32[]{:S(2)}, u32[]{:S(2)}) collective-permute-start(bf16[32,16,128]{2,1,0:T(8,128)(2,1)S(1)} %get-tuple-element.29.own), channel_id=1, source_target_pairs={{1,0},{3,2},{5,4},{7,6},{8,9},{10,11},{12,13},{14,15},{17,16},{19,... | collective-permute-start | bytes 393224 | tf_op jit(solution)/shard_map/ppermute | solution.py:353
  25.4 10.0 %collective-permute-start.7 = (bf16[32,16,128]{2,1,0:T(8,128)(2,1)S(1)}, bf16[32,16,128]{2,1,0:T(8,128)(2,1)S(1)}, u32[]{:S(2)}, u32[]{:S(2)}) collective-permute-start(bf16[32,16,128]{2,1,0:T(8,128)(2,1)S(1)} %get-tuple-element.30), channel_id=1, source_target_pairs={{0,2},{1,10},{2,0},{3,8},{4,6},{5,14},{6,4},{7,12},{8,3},{9,11},{1... | collective-permute-start | bytes 393224 | tf_op jit(solution)/shard_map/ppermute | solution.py:353
  25.5 9.9 %collective-permute-start.8 = (bf16[32,16,128]{2,1,0:T(8,128)(2,1)S(1)}, bf16[32,16,128]{2,1,0:T(8,128)(2,1)S(1)}, u32[]{:S(2)}, u32[]{:S(2)}) collective-permute-start(bf16[32,16,128]{2,1,0:T(8,128)(2,1)S(1)} %get-tuple-element.31), channel_id=1, source_target_pairs={{0,4},{1,12},{2,6},{3,14},{4,0},{5,8},{6,2},{7,10},{8,5},{9,13},{1... | collective-permute-start | bytes 393224 | tf_op jit(solution)/shard_map/ppermute | solution.py:353
  27.7 14.9 %collective-permute-start.9 = (bf16[32,16,128]{2,1,0:T(8,128)(2,1)S(1)}, bf16[32,16,128]{2,1,0:T(8,128)(2,1)S(1)}, u32[]{:S(2)}, u32[]{:S(2)}) collective-permute-start(bf16[32,16,128]{2,1,0:T(8,128)(2,1)S(1)} %get-tuple-element.32), channel_id=1, source_target_pairs={{0,6},{1,14},{2,4},{3,12},{4,2},{5,10},{6,0},{7,8},{8,7},{9,15},{1... | collective-permute-start | bytes 393224 | tf_op jit(solution)/shard_map/ppermute | solution.py:353
  30.1 12.5 %collective-permute-start.6 = (bf16[32,16,128]{2,1,0:T(8,128)(2,1)S(1)}, bf16[32,16,128]{2,1,0:T(8,128)(2,1)S(1)}, u32[]{:S(2)}, u32[]{:S(2)}) collective-permute-start(bf16[32,16,128]{2,1,0:T(8,128)(2,1)S(1)} %collective-permute-done.5), channel_id=1, source_target_pairs={{0,8},{2,10},{4,12},{6,14},{9,1},{11,3},{13,5},{15,7},{16,24},{18,... | collective-permute-start | bytes 393224 | tf_op jit(solution)/shard_map/ppermute | solution.py:353
  43.5 15.5 %collective-permute-start.10 = (bf16[24,64,128]{2,1,0:T(8,128)(2,1)S(1)}, bf16[24,64,128]{2,1,0:T(8,128)(2,1)S(1)}, u32[]{:S(2)}, u32[]{:S(2)}) collective-permute-start(bf16[24,64,128]{2,1,0:T(8,128)(2,1)S(1)} %get-tuple-element.34), channel_id=1, source_target_pairs={{0,2},{1,3},{2,0},{3,1},{4,6},{5,7},{6,4},{7,5},{8,10},{9,11},{10,... | collective-permute-start | bytes 1179656 | tf_op jit(solution)/shard_map/ppermute | solution.py:335
  43.7 15.3 %collective-permute-start.11 = (bf16[24,64,128]{2,1,0:T(8,128)(2,1)S(1)}, bf16[24,64,128]{2,1,0:T(8,128)(2,1)S(1)}, u32[]{:S(2)}, u32[]{:S(2)}) collective-permute-start(bf16[24,64,128]{2,1,0:T(8,128)(2,1)S(1)} %get-tuple-element.35), channel_id=1, source_target_pairs={{2,4},{3,5},{4,2},{5,3},{6,8},{7,9},{8,6},{9,7},{10,12},{11,13},{1... | collective-permute-start | bytes 1179656 | tf_op jit(solution)/shard_map/ppermute | solution.py:335
  45.8 13.2 %collective-permute-start.12 = (bf16[7,64,128]{2,1,0:T(8,128)(2,1)S(1)}, bf16[7,64,128]{2,1,0:T(8,128)(2,1)S(1)}, u32[]{:S(2)}, u32[]{:S(2)}) collective-permute-start(bf16[7,64,128]{2,1,0:T(8,128)(2,1)S(1)} %get-tuple-element.36), channel_id=1, source_target_pairs={{0,1},{1,0},{2,3},{3,2},{4,5},{5,4},{6,7},{7,6},{8,9},{9,8},{10,11... | collective-permute-start | bytes 344072 | tf_op jit(solution)/shard_map/ppermute | solution.py:335
  52.4 3.9 %collective-permute-start.13 = (bf16[5,64,128]{2,1,0:T(8,128)(2,1)S(1)}, bf16[5,64,128]{2,1,0:T(8,128)(2,1)S(1)}, u32[]{:S(2)}, u32[]{:S(2)}) collective-permute-start(bf16[5,64,128]{2,1,0:T(8,128)(2,1)S(1)} %get-tuple-element.37), channel_id=1, source_target_pairs={{0,3},{1,2},{2,1},{3,0},{4,7},{5,6},{6,5},{7,4},{8,11},{9,10},{10,... | collective-permute-start | bytes 245768 | tf_op jit(solution)/shard_map/ppermute | solution.py:335
  52.4 6.6 %collective-permute-start.14 = (bf16[5,64,128]{2,1,0:T(8,128)(2,1)S(1)}, bf16[5,64,128]{2,1,0:T(8,128)(2,1)S(1)}, u32[]{:S(2)}, u32[]{:S(2)}) collective-permute-start(bf16[5,64,128]{2,1,0:T(8,128)(2,1)S(1)} %get-tuple-element.38), channel_id=1, source_target_pairs={{2,5},{3,4},{4,3},{5,2},{6,9},{7,8},{8,7},{9,6},{10,13},{11,12},{1... | collective-permute-start | bytes 245768 | tf_op jit(solution)/shard_map/ppermute | solution.py:335

commit v2 on v1

--- a/solution.py
+++ b/solution.py
@@ -107,7 +107,7 @@
 SLOT = 32
 FULL = ROWS + 2 * HALO
 KDIM = 3 * CH + 16
-UNROLL = 16
+UNROLL = 24
 BF16 = jnp.bfloat16
 F32 = jnp.float32
 
@@ -117,44 +117,43 @@
     return r, c, lax.rem(r, 2)
 
 
-def edge_groups(rows):
-    return -(-rows // EDGE_SLOTS)
-
-
-def edge_pack(row_of, out_ref, c, start, rows):
-    lane = lax.broadcasted_iota(jnp.int32, (CH, COLS), 1)
-    groups = edge_groups(rows)
-    for t in range(groups):
-        acc = None
-        for q in range(EDGE_SLOTS):
-            i = t + groups * q
-            if i < rows:
-                piece = pltpu.roll(row_of(start + i), lax.rem(HALO * (q + 1 - c) + c * COLS, COLS), 1)
-                acc = piece if acc is None else jnp.where(lane >= HALO * q, piece, acc)
-        out_ref[t] = acc.astype(BF16)
-
-
-def pack_sends(read, a_ref, b_ref, c_ref, d_ref, e_ref, c, core):
+EDGE_GROUPS = -(-ROWS // EDGE_SLOTS)
+
+
+def pack_sends(read, a_ref, b_ref, c_ref, c, core):
     off_a = (ROWS - HALO) * (1 - core)
     off_b = (ROWS - HALO) * core
     for i in range(HALO):
         a_ref[i] = read(off_a + i)
         b_ref[i] = read(off_b + i)
-
-    def row_of(i):
-        return read(i).astype(F32)
-
-    edge_pack(row_of, c_ref, c, 0, ROWS)
-    edge_pack(row_of, d_ref, c, off_a, HALO)
-    edge_pack(row_of, e_ref, c, off_b, HALO)
-
-
-def pack_kernel(x_ref, xt_ref, a_ref, b_ref, c_ref, d_ref, e_ref, flat):
+    lane = lax.broadcasted_iota(jnp.int32, (CH, COLS), 1)
+    for t in range(EDGE_GROUPS):
+        acc = None
+        for q in range(EDGE_SLOTS):
+            i = t + EDGE_GROUPS * q
+            if i < ROWS:
+                piece = pltpu.roll(read(i), lax.rem(HALO * (q + 1 - c) + c * COLS, COLS), 1)
+                acc = piece if acc is None else jnp.where(lane >= HALO * q, piece, acc)
+        c_ref[t] = acc
+
+
+CHUNK = 16
+
+
+def pack_kernel(x_ref, xt_ref, a_ref, b_ref, c_ref, raw, flat, sems):
     _, c, core = place()
-    flat[...] = x_ref[...].reshape(CH * ROWS, COLS).astype(F32)
-    for h in range(ROWS):
-        xt_ref[h] = flat[pl.ds(h, CH, stride=ROWS), :].astype(BF16)
-    pack_sends(lambda i: xt_ref[i], a_ref, b_ref, c_ref, d_ref, e_ref, c, core)
+    copies = []
+    for k in range(CH // CHUNK):
+        part = pl.ds(k * CHUNK, CHUNK)
+        copies.append(pltpu.make_async_copy(x_ref.at[part], raw.at[part], sems.at[k]))
+        copies[k].start()
+    for k, copy in enumerate(copies):
+        copy.wait()
+        first = k * CHUNK
+        flat[first * ROWS : (first + CHUNK) * ROWS, :] = raw[first : first + CHUNK].reshape(CHUNK * ROWS, COLS).astype(F32)
+        for h in range(ROWS):
+            xt_ref[h, first : first + CHUNK, :] = flat[pl.ds(first * ROWS + h, CHUNK, stride=ROWS), :].astype(BF16)
+    pack_sends(lambda i: xt_ref[i], a_ref, b_ref, c_ref, c, core)
 
 
 def assemble(xa, xt_ref, a_ref, b_ref, c_ref, d_ref, e_ref, c, core):
@@ -168,15 +167,13 @@
     for i in range(HALO):
         xa[at_a + i, :, 0:COLS] = a_ref[i]
         xa[at_b + i, :, 0:COLS] = b_ref[i]
-    for ref, start, rows in ((c_ref, HALO, ROWS), (d_ref, at_a, HALO), (e_ref, at_b, HALO)):
-        groups = edge_groups(rows)
-        for t in range(groups):
-            packed = ref[t].astype(F32)
-            for q in range(EDGE_SLOTS):
-                i = t + groups * q
-                if i < rows:
-                    piece = pltpu.roll(packed, lax.rem(COLS + first - HALO * q, COLS), 1)
-                    xa[start + i, :, COLS:] = jnp.where(mask, piece, 0.0).astype(BF16)
+    nil = jnp.zeros((CH, COLS), BF16)
+    other = ROWS - HALO
+    for ref, start, skip, rows in ((c_ref, HALO, 0, ROWS), (d_ref, at_a, other * core, HALO), (e_ref, at_b, other * (1 - core), HALO)):
+        for i in range(rows):
+            t, q = lax.rem(i + skip, EDGE_GROUPS), lax.div(i + skip, EDGE_GROUPS)
+            piece = pltpu.roll(ref[t], lax.rem(COLS + first - HALO * q, COLS), 1)
+            xa[start + i, :, COLS:] = jnp.where(mask, piece, nil)
     return mask
 
 
@@ -221,13 +218,18 @@
                 else:
                     dst[h, :, COLS:] = jnp.where(mask, new, 0.0).astype(BF16)
 
-        def step(i, _, lo=lo, hi=hi, row=row):
-            first = jnp.minimum(lo + i * UNROLL, hi - UNROLL)
-            for u in range(UNROLL):
+        rows = ROWS if final else UNROLL
+
+        def step(i, _, lo=lo, hi=hi, row=row, rows=rows):
+            first = jnp.minimum(lo + i * rows, hi - rows)
+            for u in range(rows):
                 row(first + u)
             return 0
 
-        lax.fori_loop(0, (hi - lo + UNROLL - 1) // UNROLL, step, 0)
+        if final:
+            step(0, 0)
+        else:
+            lax.fori_loop(0, lax.div(hi - lo + rows - 1, rows), step, 0)
         src, dst = dst, src
 
 
@@ -266,7 +268,7 @@
         ref[...] = turned[pl.ds(start, ROWS * 16), :].reshape(ROWS, 16, COLS).astype(BF16)
 
 
-def mirror_kernel(x_ref, own, m0, m1, m2, m3, xt_ref, a_ref, b_ref, c_ref, d_ref, e_ref, got):
+def mirror_kernel(x_ref, own, m0, m1, m2, m3, xt_ref, a_ref, b_ref, c_ref, got):
     r, c, core = place()
     rr = lax.rem(r, 4)
     for k, ref in enumerate((m0, m1, m2, m3)):
@@ -285,7 +287,7 @@
         return out
 
     for i in range(ROWS):
-        parts = [got[q, i].astype(F32) for q in range(4)]
+        parts = [got[q, i] for q in range(4)]
         moved = []
         for d in range(4):
             v = by_slot([parts[(q + d) % 4] for q in range(4)])
@@ -293,8 +295,8 @@
         mirrored = jnp.concatenate(
             [by_slot([moved[(q - k) % 4] for q in range(4)]) for k in range(4)], axis=0
         )
-        xt_ref[i] = (0.5 * (x_ref[i].astype(F32) + mirrored)).astype(BF16)
-    pack_sends(lambda i: xt_ref[i], a_ref, b_ref, c_ref, d_ref, e_ref, c, core)
+        xt_ref[i] = (0.5 * (x_ref[i].astype(F32) + mirrored.astype(F32))).astype(BF16)
+    pack_sends(lambda i: xt_ref[i], a_ref, b_ref, c_ref, c, core)
 
 
 def second_kernel(row_count, dil_ref, w_ref, xt_ref, a_ref, b_ref, c_ref, d_ref, e_ref, o_ref, xa, xb, flat):
@@ -308,22 +310,21 @@
     o_ref[...] = flat[...].reshape(CH, ROWS, COLS).astype(BF16)
 
 
-def kernel_call(body, outs, scratch, operands, smem=0, cost=None):
+def kernel_call(body, outs, scratch, operands, smem=0, anywhere=0):
     vmem = pl.BlockSpec(memory_space=pltpu.VMEM)
     return pl.pallas_call(
         body,
         out_shape=[jax.ShapeDtypeStruct(shape, BF16) for shape in outs],
-        in_specs=[pl.BlockSpec(memory_space=pltpu.SMEM)] * smem + [vmem] * (len(operands) - smem),
+        in_specs=[pl.BlockSpec(memory_space=pltpu.SMEM)] * smem
+        + [pl.BlockSpec(memory_space=pl.ANY)] * anywhere
+        + [vmem] * (len(operands) - smem - anywhere),
         out_specs=[vmem] * len(outs),
-        scratch_shapes=[pltpu.VMEM(shape, dtype) for shape, dtype in scratch],
+        scratch_shapes=[pltpu.VMEM(*x) if isinstance(x, tuple) else x for x in scratch],
         compiler_params=pltpu.CompilerParams(vmem_limit_bytes=48 << 20),
-        cost_estimate=cost,
     )(*operands)
 
 
-ROW_SENDS = [(HALO, CH, COLS)] * 2
-EDGE_SENDS = [(edge_groups(rows), CH, COLS) for rows in (ROWS, HALO, HALO)]
-SENDS = ROW_SENDS + EDGE_SENDS
+SENDS = [(HALO, CH, COLS), (HALO, CH, COLS), (EDGE_GROUPS, CH, COLS)]
 TILE = (ROWS, CH, COLS)
 
 
@@ -334,14 +335,11 @@
         perm = [(2 * r + c, 2 * partner(r, c)[0] + partner(r, c)[1]) for r, c in both if 0 <= partner(r, c)[0] < row_count]
         return lax.ppermute(x, ("row", "col"), perm)
 
-    a, b, c, d, e = sends
-    across = lambda r: r - 1 if r % 2 == 0 else r + 1
-    got_e = swap(e, lambda r, c: (across(r), 1 - c))
-    got_b = swap(b, lambda r, c: (across(r), c))
-    got_c = swap(c, lambda r, c: (r, 1 - c))
-    got_d = swap(d, lambda r, c: (r ^ 1, 1 - c))
-    got_a = swap(a, lambda r, c: (r ^ 1, c))
-    return got_a, got_b, got_c, got_d, got_e
+    a, b, c = sends
+    chip = lambda r, c: (r ^ 1, c)
+    across = lambda r, c: (r - 1 if r % 2 == 0 else r + 1, c)
+    got_a, got_b, got_c = swap(a, chip), swap(b, across), swap(c, lambda r, c: (r, 1 - c))
+    return got_a, got_b, got_c, swap(got_c, chip), swap(got_c, across)
 
 
 def swap_mirror(blocks, row_count):
@@ -359,7 +357,13 @@
 
 def on_tile(row_count, maps, weights, biases, dilations):
     (matrices,) = kernel_call(weights_kernel, [(LAYERS, 3 * CH, KDIM)], [], [weights, biases])
-    tile, *sends = kernel_call(pack_kernel, [TILE] + SENDS, [((CH * ROWS, COLS), F32)], [maps])
+    tile, *sends = kernel_call(
+        pack_kernel,
+        [TILE] + SENDS,
+        [((CH, ROWS, COLS), BF16), ((CH * ROWS, COLS), F32), pltpu.SemaphoreType.DMA((CH // CHUNK,))],
+        [maps],
+        anywhere=1,
+    )
     halos = swap_halos(sends, row_count)
     work = [((FULL, CH, 2 * COLS), BF16)] * 2 + [((CH * ROWS, COLS), F32)]
     tile, *blocks = kernel_call(

time: 69.4 us -> 73.5 us (1.059)
  starting transfers between devices: 32.3 us -> 36.4 us
    ppermute x10, waiting for transfers between devices: 3.09 us -> 7.8 us  [swap(): return lax.ppermute(x, ('row', 'col'), perm)]
    ppermute x10, starting transfers between devices: 23.3 us -> 27.6 us  [swap(): return lax.ppermute(x, ('row', 'col'), perm)]
    ppermute x5, waiting for transfers between devices: 9.55 us -> 5.34 us  [send(): lax.ppermute(x, ('row', 'col'), [(2 * r + c, 2 * target(r, c)[0] + target...]
  transfers between devices with their start and end apart: 15 -> 15, of which waited for: 4 -> 7; matrix products, arithmetic and copies ran while one was open for 0% -> 0% of each run, Pallas kernels for 1% -> 1%
where the time goes in v2:
time: 73.5 us; the launch traced here: 72.9 us
  starting transfers between devices  36.4 us (50%)
  Pallas kernels  21 us (29%)
  waiting for transfers between devices  13.1 us (18%)
  local copies, waits for them, and re-layouts  2.22 us (3%)
    ppermute x10, starting transfers between devices, swap(): return lax.ppermute(x, ('row', 'col'), perm)  27.6 us
    pallas_call x5, Pallas kernels, kernel_call(): pl.pallas_call(body, out_shape=[jax.ShapeDtypeStruct(shape, BF16) for sha...  21 us
    ppermute x5, starting transfers between devices, send(): lax.ppermute(x, ('row', 'col'), [(2 * r + c, 2 * target(r, c)[0] + target...  8.78 us
    ppermute x10, waiting for transfers between devices, swap(): return lax.ppermute(x, ('row', 'col'), perm)  7.8 us
    ppermute x5, waiting for transfers between devices, send(): lax.ppermute(x, ('row', 'col'), [(2 * r + c, 2 * target(r, c)[0] + target...  5.34 us
    unnamed x8, local copies, waits for them, and re-layouts  2.22 us
  transfers between devices with their start and end apart: 15, of which 7 were waited for; matrix products, arithmetic and copies ran while one was open for 0% of the time, Pallas kernels for 1%

profile of v2, /device:TPU:1, one launch (start us, length us, event | category | flops | bytes accessed | tf_op | source)
XLA Modules:
  0.0 72.9 jit_solution(3630816060970437967)
XLA Ops:
  0.0 1.0 %copy-done.1 = bf16[64,32,128]{2,1,0:T(8,128)(2,1)S(1)} copy-done((bf16[64,32,128]{2,1,0:T(8,128)(2,1)S(1)}, bf16[64,32,128]{2,1,0:T(8,128)(2,1)}, u32[]{:S(2)}) %copy-start.1) | copy-done | bytes 524312
  1.0 1.6 %shard_map.47 = (bf16[32,64,128]{2,1,0:T(8,128)(2,1)S(1)}, bf16[24,64,128]{2,1,0:T(8,128)(2,1)S(1)}, bf16[24,64,128]{2,1,0:T(8,128)(2,1)S(1)}, bf16[7,64,128]{2,1,0:T(8,128)(2,1)S(1)}) custom-call(bf16[64,32,128]{2,1,0:T(8,128)(2,1)S(1)} %copy-done.1), custom_call_target="tpu_custom_call" | custom-call | tf_op jit(solution)/shard_map/pallas_call | solution.py:315
  2.6 0.0 copy-start.2
  2.6 0.1 collective-permute-start
  2.7 4.6 %collective-permute-start.1 = (bf16[24,64,128]{2,1,0:T(8,128)(2,1)S(1)}, bf16[24,64,128]{2,1,0:T(8,128)(2,1)S(1)}, u32[]{:S(2)}, u32[]{:S(2)}) collective-permute-start(bf16[24,64,128]{2,1,0:T(8,128)(2,1)S(1)} %get-tuple-element.20), channel_id=1, source_target_pairs={{2,4},{3,5},{4,2},{5,3},{6,8},{7,9},{8,6},{9,7},{10,12},{11,13},{1... | collective-permute-start | bytes 1179656 | tf_op jit(solution)/shard_map/ppermute | solution.py:336
  7.3 1.3 %collective-permute-start.2 = (bf16[7,64,128]{2,1,0:T(8,128)(2,1)S(1)}, bf16[7,64,128]{2,1,0:T(8,128)(2,1)S(1)}, u32[]{:S(2)}, u32[]{:S(2)}) collective-permute-start(bf16[7,64,128]{2,1,0:T(8,128)(2,1)S(1)} %get-tuple-element.21), channel_id=1, source_target_pairs={{0,1},{1,0},{2,3},{3,2},{4,5},{5,4},{6,7},{7,6},{8,9},{9,8},{10,11... | collective-permute-start | bytes 344072 | tf_op jit(solution)/shard_map/ppermute | solution.py:336
  8.6 2.4 %collective-permute-done.2.c_ref = bf16[7,64,128]{2,1,0:T(8,128)(2,1)S(1)} collective-permute-done((bf16[7,64,128]{2,1,0:T(8,128)(2,1)S(1)}, bf16[7,64,128]{2,1,0:T(8,128)(2,1)S(1)}, u32[]{:S(2)}, u32[]{:S(2)}) %collective-permute-start.2) | collective-permute-done | bytes 114720 | tf_op jit(solution)/shard_map/ppermute | solution.py:336
  11.0 3.6 %collective-permute-start.4 = (bf16[7,64,128]{2,1,0:T(8,128)(2,1)S(1)}, bf16[7,64,128]{2,1,0:T(8,128)(2,1)S(1)}, u32[]{:S(2)}, u32[]{:S(2)}) collective-permute-start(bf16[7,64,128]{2,1,0:T(8,128)(2,1)S(1)} %collective-permute-done.2.c_ref), channel_id=1, source_target_pairs={{2,4},{3,5},{4,2},{5,3},{6,8},{7,9},{8,6},{9,7},{10,12},{11,13},{1... | collective-permute-start | bytes 344072 | tf_op jit(solution)/shard_map/ppermute | solution.py:336
  14.7 0.1 collective-permute-start.3
  14.7 0.0 copy-start
  14.8 1.2 %copy-done = bf16[6,3,3,64,64]{4,3,2,1,0:T(8,128)(2,1)S(1)} copy-done((bf16[6,3,3,64,64]{4,3,2,1,0:T(8,128)(2,1)S(1)}, bf16[6,3,3,64,64]{4,3,2,1,0:T(8,128)(2,1)}, u32[]{:S(2)}) %copy-start) | copy-done | bytes 442392
  15.9 0.5 shard_map.46.w_ref
  16.5 0.0 copy-start.3
  16.5 0.6 collective-permute-done.4.e_ref
  17.1 9.5 %shard_map.48 = (bf16[32,64,128]{2,1,0:T(8,128)(2,1)S(1)}, bf16[32,16,128]{2,1,0:T(8,128)(2,1)S(1)}, bf16[32,16,128]{2,1,0:T(8,128)(2,1)S(1)}, bf16[32,16,128]{2,1,0:T(8,128)(2,1)S(1)}, bf16[32,16,128]{2,1,0:T(8,128)(2,1)S(1)}) custom-call(s32[6]{0:T(128)S(1)} %copy-done.3, bf16[6,192,208]{2,1,0:T(8,128)(2,1)S(1)} %shard_map.46.w_ref, ...), custom_call_target="tpu_custom_call" | custom-call | tf_op jit(solution)/shard_map/pallas_call | solution.py:315
  26.6 1.3 %collective-permute-start.5 = (bf16[32,16,128]{2,1,0:T(8,128)(2,1)S(1)}, bf16[32,16,128]{2,1,0:T(8,128)(2,1)S(1)}, u32[]{:S(2)}, u32[]{:S(2)}) collective-permute-start(bf16[32,16,128]{2,1,0:T(8,128)(2,1)S(1)} %get-tuple-element.23.own), channel_id=1, source_target_pairs={{1,0},{3,2},{5,4},{7,6},{8,9},{10,11},{12,13},{14,15},{17,16},{19,... | collective-permute-start | bytes 393224 | tf_op jit(solution)/shard_map/ppermute | solution.py:351
  27.9 0.1 collective-permute-start.7
  28.0 2.7 %collective-permute-start.8 = (bf16[32,16,128]{2,1,0:T(8,128)(2,1)S(1)}, bf16[32,16,128]{2,1,0:T(8,128)(2,1)S(1)}, u32[]{:S(2)}, u32[]{:S(2)}) collective-permute-start(bf16[32,16,128]{2,1,0:T(8,128)(2,1)S(1)} %get-tuple-element.25), channel_id=1, source_target_pairs={{0,4},{1,12},{2,6},{3,14},{4,0},{5,8},{6,2},{7,10},{8,5},{9,13},{1... | collective-permute-start | bytes 393224 | tf_op jit(solution)/shard_map/ppermute | solution.py:351
  30.7 0.0 collective-permute-start.9
  30.8 3.0 %collective-permute-done.5 = bf16[32,16,128]{2,1,0:T(8,128)(2,1)S(1)} collective-permute-done((bf16[32,16,128]{2,1,0:T(8,128)(2,1)S(1)}, bf16[32,16,128]{2,1,0:T(8,128)(2,1)S(1)}, u32[]{:S(2)}, u32[]{:S(2)}) %collective-permute-start.5) | collective-permute-done | bytes 131104 | tf_op jit(solution)/shard_map/ppermute | solution.py:351
  33.8 4.6 %collective-permute-start.6 = (bf16[32,16,128]{2,1,0:T(8,128)(2,1)S(1)}, bf16[32,16,128]{2,1,0:T(8,128)(2,1)S(1)}, u32[]{:S(2)}, u32[]{:S(2)}) collective-permute-start(bf16[32,16,128]{2,1,0:T(8,128)(2,1)S(1)} %collective-permute-done.5), channel_id=1, source_target_pairs={{0,8},{2,10},{4,12},{6,14},{9,1},{11,3},{13,5},{15,7},{16,24},{18,... | collective-permute-start | bytes 393224 | tf_op jit(solution)/shard_map/ppermute | solution.py:351
  38.5 0.2 collective-permute-done.9.m3
  38.7 2.1 %collective-permute-done.6.m0 = bf16[32,16,128]{2,1,0:T(8,128)(2,1)S(1)} collective-permute-done((bf16[32,16,128]{2,1,0:T(8,128)(2,1)S(1)}, bf16[32,16,128]{2,1,0:T(8,128)(2,1)S(1)}, u32[]{:S(2)}, u32[]{:S(2)}) %collective-permute-start.6) | collective-permute-done | bytes 131104 | tf_op jit(solution)/shard_map/ppermute | solution.py:351
  40.8 0.6 shard_map.49
  41.4 1.4 %collective-permute-start.10 = (bf16[24,64,128]{2,1,0:T(8,128)(2,1)S(1)}, bf16[24,64,128]{2,1,0:T(8,128)(2,1)S(1)}, u32[]{:S(2)}, u32[]{:S(2)}) collective-permute-start(bf16[24,64,128]{2,1,0:T(8,128)(2,1)S(1)} %get-tuple-element.28), channel_id=1, source_target_pairs={{0,2},{1,3},{2,0},{3,1},{4,6},{5,7},{6,4},{7,5},{8,10},{9,11},{10,... | collective-permute-start | bytes 1179656 | tf_op jit(solution)/shard_map/ppermute | solution.py:336
  42.9 5.8 %collective-permute-start.11 = (bf16[24,64,128]{2,1,0:T(8,128)(2,1)S(1)}, bf16[24,64,128]{2,1,0:T(8,128)(2,1)S(1)}, u32[]{:S(2)}, u32[]{:S(2)}) collective-permute-start(bf16[24,64,128]{2,1,0:T(8,128)(2,1)S(1)} %get-tuple-element.29), channel_id=1, source_target_pairs={{2,4},{3,5},{4,2},{5,3},{6,8},{7,9},{8,6},{9,7},{10,12},{11,13},{1... | collective-permute-start | bytes 1179656 | tf_op jit(solution)/shard_map/ppermute | solution.py:336
  48.7 7.2 %collective-permute-start.12 = (bf16[7,64,128]{2,1,0:T(8,128)(2,1)S(1)}, bf16[7,64,128]{2,1,0:T(8,128)(2,1)S(1)}, u32[]{:S(2)}, u32[]{:S(2)}) collective-permute-start(bf16[7,64,128]{2,1,0:T(8,128)(2,1)S(1)} %get-tuple-element.30), channel_id=1, source_target_pairs={{0,1},{1,0},{2,3},{3,2},{4,5},{5,4},{6,7},{7,6},{8,9},{9,8},{10,11... | collective-permute-start | bytes 344072 | tf_op jit(solution)/shard_map/ppermute | solution.py:336
  55.9 2.2 %collective-permute-done.12.c_ref = bf16[7,64,128]{2,1,0:T(8,128)(2,1)S(1)} collective-permute-done((bf16[7,64,128]{2,1,0:T(8,128)(2,1)S(1)}, bf16[7,64,128]{2,1,0:T(8,128)(2,1)S(1)}, u32[]{:S(2)}, u32[]{:S(2)}) %collective-permute-start.12) | collective-permute-done | bytes 114720 | tf_op jit(solution)/shard_map/ppermute | solution.py:336
  58.0 3.5 %collective-permute-start.14 = (bf16[7,64,128]{2,1,0:T(8,128)(2,1)S(1)}, bf16[7,64,128]{2,1,0:T(8,128)(2,1)S(1)}, u32[]{:S(2)}, u32[]{:S(2)}) collective-permute-start(bf16[7,64,128]{2,1,0:T(8,128)(2,1)S(1)} %collective-permute-done.12.c_ref), channel_id=1, source_target_pairs={{2,4},{3,5},{4,2},{5,3},{6,8},{7,9},{8,6},{9,7},{10,12},{11,13},{1... | collective-permute-start | bytes 344072 | tf_op jit(solution)/shard_map/ppermute | solution.py:336
  61.5 0.1 collective-permute-start.13
  61.6 2.5 %collective-permute-done.14.e_ref = bf16[7,64,128]{2,1,0:T(8,128)(2,1)S(1)} collective-permute-done((bf16[7,64,128]{2,1,0:T(8,128)(2,1)S(1)}, bf16[7,64,128]{2,1,0:T(8,128)(2,1)S(1)}, u32[]{:S(2)}, u32[]{:S(2)}) %collective-permute-start.14) | collective-permute-done | bytes 114720 | tf_op jit(solution)/shard_map/ppermute | solution.py:336
  64.1 8.7 %shard_map.50 = bf16[64,32,128]{2,1,0:T(8,128)(2,1)} custom-call(s32[6]{0:T(128)S(1)} %copy-done.3, bf16[6,192,208]{2,1,0:T(8,128)(2,1)S(1)} %shard_map.46.w_ref, bf16[32,64,128]{2,1,0:T(8,128)(2,1)S(1)} %get-tuple-element.27.xt_ref, bf16[24,64,128]{2,1,0:T(8,128)(2,1)S(1)} %collective-permute-done.10.a_ref, ...), custom_call_target="tpu_custom_call" | custom-call | tf_op jit(solution)/shard_map/pallas_call | solution.py:315
  (11 shorter events, 0.0 us)
Async XLA Ops:
  0.0 1.0 %copy-start.1 = (bf16[64,32,128]{2,1,0:T(8,128)(2,1)S(1)}, bf16[64,32,128]{2,1,0:T(8,128)(2,1)}, u32[]{:S(2)}) copy-start(bf16[64,32,128]{2,1,0:T(8,128)(2,1)} %x_ref.1) | copy-start | bytes 1572868
  2.6 12.1 %copy-start.2 = (bf16[6,64]{1,0:T(8,128)(2,1)S(1)}, bf16[6,64]{1,0:T(8,128)(2,1)}, u32[]{:S(2)}) copy-start(bf16[6,64]{1,0:T(8,128)(2,1)} %bias_ref.1) | copy-start | bytes 2308
  2.6 14.5 %collective-permute-start = (bf16[24,64,128]{2,1,0:T(8,128)(2,1)S(1)}, bf16[24,64,128]{2,1,0:T(8,128)(2,1)S(1)}, u32[]{:S(2)}, u32[]{:S(2)}) collective-permute-start(bf16[24,64,128]{2,1,0:T(8,128)(2,1)S(1)} %get-tuple-element.19), channel_id=1, source_target_pairs={{0,2},{1,3},{2,0},{3,1},{4,6},{5,7},{6,4},{7,5},{8,10},{9,11},{10,... | collective-permute-start | bytes 1179656 | tf_op jit(solution)/shard_map/ppermute | solution.py:336
  2.7 14.4 %collective-permute-start.1 = (bf16[24,64,128]{2,1,0:T(8,128)(2,1)S(1)}, bf16[24,64,128]{2,1,0:T(8,128)(2,1)S(1)}, u32[]{:S(2)}, u32[]{:S(2)}) collective-permute-start(bf16[24,64,128]{2,1,0:T(8,128)(2,1)S(1)} %get-tuple-element.20), channel_id=1, source_target_pairs={{2,4},{3,5},{4,2},{5,3},{6,8},{7,9},{8,6},{9,7},{10,12},{11,13},{1... | collective-permute-start | bytes 1179656 | tf_op jit(solution)/shard_map/ppermute | solution.py:336
  7.3 3.7 %collective-permute-start.2 = (bf16[7,64,128]{2,1,0:T(8,128)(2,1)S(1)}, bf16[7,64,128]{2,1,0:T(8,128)(2,1)S(1)}, u32[]{:S(2)}, u32[]{:S(2)}) collective-permute-start(bf16[7,64,128]{2,1,0:T(8,128)(2,1)S(1)} %get-tuple-element.21), channel_id=1, source_target_pairs={{0,1},{1,0},{2,3},{3,2},{4,5},{5,4},{6,7},{7,6},{8,9},{9,8},{10,11... | collective-permute-start | bytes 344072 | tf_op jit(solution)/shard_map/ppermute | solution.py:336
  11.0 6.1 %collective-permute-start.4 = (bf16[7,64,128]{2,1,0:T(8,128)(2,1)S(1)}, bf16[7,64,128]{2,1,0:T(8,128)(2,1)S(1)}, u32[]{:S(2)}, u32[]{:S(2)}) collective-permute-start(bf16[7,64,128]{2,1,0:T(8,128)(2,1)S(1)} %collective-permute-done.2.c_ref), channel_id=1, source_target_pairs={{2,4},{3,5},{4,2},{5,3},{6,8},{7,9},{8,6},{9,7},{10,12},{11,13},{1... | collective-permute-start | bytes 344072 | tf_op jit(solution)/shard_map/ppermute | solution.py:336
  14.7 2.5 %collective-permute-start.3 = (bf16[7,64,128]{2,1,0:T(8,128)(2,1)S(1)}, bf16[7,64,128]{2,1,0:T(8,128)(2,1)S(1)}, u32[]{:S(2)}, u32[]{:S(2)}) collective-permute-start(bf16[7,64,128]{2,1,0:T(8,128)(2,1)S(1)} %collective-permute-done.2.c_ref), channel_id=1, source_target_pairs={{0,2},{1,3},{2,0},{3,1},{4,6},{5,7},{6,4},{7,5},{8,10},{9,11},{10,... | collective-permute-start | bytes 344072 | tf_op jit(solution)/shard_map/ppermute | solution.py:336
  14.7 1.2 %copy-start = (bf16[6,3,3,64,64]{4,3,2,1,0:T(8,128)(2,1)S(1)}, bf16[6,3,3,64,64]{4,3,2,1,0:T(8,128)(2,1)}, u32[]{:S(2)}) copy-start(bf16[6,3,3,64,64]{4,3,2,1,0:T(8,128)(2,1)} %w_ref.1) | copy-start | bytes 1327108
  16.5 0.7 copy-start.3
  26.6 7.2 %collective-permute-start.5 = (bf16[32,16,128]{2,1,0:T(8,128)(2,1)S(1)}, bf16[32,16,128]{2,1,0:T(8,128)(2,1)S(1)}, u32[]{:S(2)}, u32[]{:S(2)}) collective-permute-start(bf16[32,16,128]{2,1,0:T(8,128)(2,1)S(1)} %get-tuple-element.23.own), channel_id=1, source_target_pairs={{1,0},{3,2},{5,4},{7,6},{8,9},{10,11},{12,13},{14,15},{17,16},{19,... | collective-permute-start | bytes 393224 | tf_op jit(solution)/shard_map/ppermute | solution.py:351
  27.9 10.6 %collective-permute-start.7 = (bf16[32,16,128]{2,1,0:T(8,128)(2,1)S(1)}, bf16[32,16,128]{2,1,0:T(8,128)(2,1)S(1)}, u32[]{:S(2)}, u32[]{:S(2)}) collective-permute-start(bf16[32,16,128]{2,1,0:T(8,128)(2,1)S(1)} %get-tuple-element.24), channel_id=1, source_target_pairs={{0,2},{1,10},{2,0},{3,8},{4,6},{5,14},{6,4},{7,12},{8,3},{9,11},{1... | collective-permute-start | bytes 393224 | tf_op jit(solution)/shard_map/ppermute | solution.py:351
  28.0 10.5 %collective-permute-start.8 = (bf16[32,16,128]{2,1,0:T(8,128)(2,1)S(1)}, bf16[32,16,128]{2,1,0:T(8,128)(2,1)S(1)}, u32[]{:S(2)}, u32[]{:S(2)}) collective-permute-start(bf16[32,16,128]{2,1,0:T(8,128)(2,1)S(1)} %get-tuple-element.25), channel_id=1, source_target_pairs={{0,4},{1,12},{2,6},{3,14},{4,0},{5,8},{6,2},{7,10},{8,5},{9,13},{1... | collective-permute-start | bytes 393224 | tf_op jit(solution)/shard_map/ppermute | solution.py:351
  30.7 7.9 %collective-permute-start.9 = (bf16[32,16,128]{2,1,0:T(8,128)(2,1)S(1)}, bf16[32,16,128]{2,1,0:T(8,128)(2,1)S(1)}, u32[]{:S(2)}, u32[]{:S(2)}) collective-permute-start(bf16[32,16,128]{2,1,0:T(8,128)(2,1)S(1)} %get-tuple-element.26), channel_id=1, source_target_pairs={{0,6},{1,14},{2,4},{3,12},{4,2},{5,10},{6,0},{7,8},{8,7},{9,15},{1... | collective-permute-start | bytes 393224 | tf_op jit(solution)/shard_map/ppermute | solution.py:351
  33.8 7.0 %collective-permute-start.6 = (bf16[32,16,128]{2,1,0:T(8,128)(2,1)S(1)}, bf16[32,16,128]{2,1,0:T(8,128)(2,1)S(1)}, u32[]{:S(2)}, u32[]{:S(2)}) collective-permute-start(bf16[32,16,128]{2,1,0:T(8,128)(2,1)S(1)} %collective-permute-done.5), channel_id=1, source_target_pairs={{0,8},{2,10},{4,12},{6,14},{9,1},{11,3},{13,5},{15,7},{16,24},{18,... | collective-permute-start | bytes 393224 | tf_op jit(solution)/shard_map/ppermute | solution.py:351
  41.4 22.7 %collective-permute-start.10 = (bf16[24,64,128]{2,1,0:T(8,128)(2,1)S(1)}, bf16[24,64,128]{2,1,0:T(8,128)(2,1)S(1)}, u32[]{:S(2)}, u32[]{:S(2)}) collective-permute-start(bf16[24,64,128]{2,1,0:T(8,128)(2,1)S(1)} %get-tuple-element.28), channel_id=1, source_target_pairs={{0,2},{1,3},{2,0},{3,1},{4,6},{5,7},{6,4},{7,5},{8,10},{9,11},{10,... | collective-permute-start | bytes 1179656 | tf_op jit(solution)/shard_map/ppermute | solution.py:336
  42.9 21.3 %collective-permute-start.11 = (bf16[24,64,128]{2,1,0:T(8,128)(2,1)S(1)}, bf16[24,64,128]{2,1,0:T(8,128)(2,1)S(1)}, u32[]{:S(2)}, u32[]{:S(2)}) collective-permute-start(bf16[24,64,128]{2,1,0:T(8,128)(2,1)S(1)} %get-tuple-element.29), channel_id=1, source_target_pairs={{2,4},{3,5},{4,2},{5,3},{6,8},{7,9},{8,6},{9,7},{10,12},{11,13},{1... | collective-permute-start | bytes 1179656 | tf_op jit(solution)/shard_map/ppermute | solution.py:336
  48.7 9.4 %collective-permute-start.12 = (bf16[7,64,128]{2,1,0:T(8,128)(2,1)S(1)}, bf16[7,64,128]{2,1,0:T(8,128)(2,1)S(1)}, u32[]{:S(2)}, u32[]{:S(2)}) collective-permute-start(bf16[7,64,128]{2,1,0:T(8,128)(2,1)S(1)} %get-tuple-element.30), channel_id=1, source_target_pairs={{0,1},{1,0},{2,3},{3,2},{4,5},{5,4},{6,7},{7,6},{8,9},{9,8},{10,11... | collective-permute-start | bytes 344072 | tf_op jit(solution)/shard_map/ppermute | solution.py:336
  58.0 6.1 %collective-permute-start.14 = (bf16[7,64,128]{2,1,0:T(8,128)(2,1)S(1)}, bf16[7,64,128]{2,1,0:T(8,128)(2,1)S(1)}, u32[]{:S(2)}, u32[]{:S(2)}) collective-permute-start(bf16[7,64,128]{2,1,0:T(8,128)(2,1)S(1)} %collective-permute-done.12.c_ref), channel_id=1, source_target_pairs={{2,4},{3,5},{4,2},{5,3},{6,8},{7,9},{8,6},{9,7},{10,12},{11,13},{1... | collective-permute-start | bytes 344072 | tf_op jit(solution)/shard_map/ppermute | solution.py:336
  61.5 2.6 %collective-permute-start.13 = (bf16[7,64,128]{2,1,0:T(8,128)(2,1)S(1)}, bf16[7,64,128]{2,1,0:T(8,128)(2,1)S(1)}, u32[]{:S(2)}, u32[]{:S(2)}) collective-permute-start(bf16[7,64,128]{2,1,0:T(8,128)(2,1)S(1)} %collective-permute-done.12.c_ref), channel_id=1, source_target_pairs={{0,2},{1,3},{2,0},{3,1},{4,6},{5,7},{6,4},{7,5},{8,10},{9,11},{10,... | collective-permute-start | bytes 344072 | tf_op jit(solution)/shard_map/ppermute | solution.py:336

commit v3 on v2

--- a/solution.py
+++ b/solution.py
@@ -137,22 +137,11 @@
         c_ref[t] = acc
 
 
-CHUNK = 16
-
-
-def pack_kernel(x_ref, xt_ref, a_ref, b_ref, c_ref, raw, flat, sems):
+def pack_kernel(x_ref, xt_ref, a_ref, b_ref, c_ref, flat):
     _, c, core = place()
-    copies = []
-    for k in range(CH // CHUNK):
-        part = pl.ds(k * CHUNK, CHUNK)
-        copies.append(pltpu.make_async_copy(x_ref.at[part], raw.at[part], sems.at[k]))
-        copies[k].start()
-    for k, copy in enumerate(copies):
-        copy.wait()
-        first = k * CHUNK
-        flat[first * ROWS : (first + CHUNK) * ROWS, :] = raw[first : first + CHUNK].reshape(CHUNK * ROWS, COLS).astype(F32)
-        for h in range(ROWS):
-            xt_ref[h, first : first + CHUNK, :] = flat[pl.ds(first * ROWS + h, CHUNK, stride=ROWS), :].astype(BF16)
+    flat[...] = x_ref[...].reshape(CH * ROWS, COLS).astype(F32)
+    for h in range(ROWS):
+        xt_ref[h] = flat[pl.ds(h, CH, stride=ROWS), :].astype(BF16)
     pack_sends(lambda i: xt_ref[i], a_ref, b_ref, c_ref, c, core)
 
 
@@ -218,18 +207,21 @@
                 else:
                     dst[h, :, COLS:] = jnp.where(mask, new, 0.0).astype(BF16)
 
-        rows = ROWS if final else UNROLL
-
-        def step(i, _, lo=lo, hi=hi, row=row, rows=rows):
-            first = jnp.minimum(lo + i * rows, hi - rows)
-            for u in range(rows):
-                row(first + u)
-            return 0
-
         if final:
-            step(0, 0)
+            for u in range(ROWS):
+                row(lo + u)
         else:
-            lax.fori_loop(0, lax.div(hi - lo + rows - 1, rows), step, 0)
+            count = hi - lo
+            for rows, fits in ((UNROLL, count <= 2 * UNROLL), (ROWS, count > 2 * UNROLL)):
+
+                def step(i, _, lo=lo, hi=hi, row=row, rows=rows):
+                    first = jnp.minimum(lo + i * rows, hi - rows)
+                    for u in range(rows):
+                        row(first + u)
+                    return 0
+
+                if rows == UNROLL or layer == 0:
+                    lax.fori_loop(0, jnp.where(fits, lax.div(count + rows - 1, rows), 0), step, 0)
         src, dst = dst, src
 
 
@@ -310,16 +302,14 @@
     o_ref[...] = flat[...].reshape(CH, ROWS, COLS).astype(BF16)
 
 
-def kernel_call(body, outs, scratch, operands, smem=0, anywhere=0):
+def kernel_call(body, outs, scratch, operands, smem=0):
     vmem = pl.BlockSpec(memory_space=pltpu.VMEM)
     return pl.pallas_call(
         body,
         out_shape=[jax.ShapeDtypeStruct(shape, BF16) for shape in outs],
-        in_specs=[pl.BlockSpec(memory_space=pltpu.SMEM)] * smem
-        + [pl.BlockSpec(memory_space=pl.ANY)] * anywhere
-        + [vmem] * (len(operands) - smem - anywhere),
+        in_specs=[pl.BlockSpec(memory_space=pltpu.SMEM)] * smem + [vmem] * (len(operands) - smem),
         out_specs=[vmem] * len(outs),
-        scratch_shapes=[pltpu.VMEM(*x) if isinstance(x, tuple) else x for x in scratch],
+        scratch_shapes=[pltpu.VMEM(shape, dtype) for shape, dtype in scratch],
         compiler_params=pltpu.CompilerParams(vmem_limit_bytes=48 << 20),
     )(*operands)
 
@@ -357,13 +347,7 @@
 
 def on_tile(row_count, maps, weights, biases, dilations):
     (matrices,) = kernel_call(weights_kernel, [(LAYERS, 3 * CH, KDIM)], [], [weights, biases])
-    tile, *sends = kernel_call(
-        pack_kernel,
-        [TILE] + SENDS,
-        [((CH, ROWS, COLS), BF16), ((CH * ROWS, COLS), F32), pltpu.SemaphoreType.DMA((CH // CHUNK,))],
-        [maps],
-        anywhere=1,
-    )
+    tile, *sends = kernel_call(pack_kernel, [TILE] + SENDS, [((CH * ROWS, COLS), F32)], [maps])
     halos = swap_halos(sends, row_count)
     work = [((FULL, CH, 2 * COLS), BF16)] * 2 + [((CH * ROWS, COLS), F32)]
     tile, *blocks = kernel_call(

time: 73.5 us -> 73.1 us (level)
  Pallas kernels: 21 us -> 20.2 us
    pallas_call x5, Pallas kernels: 21 us -> 20.2 us  [kernel_call(): pl.pallas_call(body, out_shape=[jax.ShapeDtypeStruct(shape, BF16) for sha...]
where the time goes in v3:
time: 73.1 us; the launch traced here: 72.1 us
  starting transfers between devices  35.7 us (49%)
  Pallas kernels  20.2 us (28%)
  waiting for transfers between devices  13.8 us (19%)
  local copies, waits for them, and re-layouts  2.21 us (3%)
    ppermute x10, starting transfers between devices, swap(): return lax.ppermute(x, ('row', 'col'), perm)  27.1 us
    pallas_call x5, Pallas kernels, kernel_call(): pl.pallas_call(body, out_shape=[jax.ShapeDtypeStruct(shape, BF16) for sha...  20.2 us
    ppermute x5, starting transfers between devices, send(): lax.ppermute(x, ('row', 'col'), [(2 * r + c, 2 * target(r, c)[0] + target...  8.57 us
    ppermute x10, waiting for transfers between devices, swap(): return lax.ppermute(x, ('row', 'col'), perm)  8.27 us
    ppermute x5, waiting for transfers between devices, send(): lax.ppermute(x, ('row', 'col'), [(2 * r + c, 2 * target(r, c)[0] + target...  5.54 us
    unnamed x8, local copies, waits for them, and re-layouts  2.21 us
  transfers between devices with their start and end apart: 15, of which 7 were waited for; matrix products, arithmetic and copies ran while one was open for 0% of the time, Pallas kernels for 1%

profile of v3, /device:TPU:1, one launch (start us, length us, event | category | flops | bytes accessed | tf_op | source)
XLA Modules:
  0.0 72.1 jit_solution(5632132049733661895)
XLA Ops:
  0.0 1.0 %copy-done.1 = bf16[64,32,128]{2,1,0:T(8,128)(2,1)S(1)} copy-done((bf16[64,32,128]{2,1,0:T(8,128)(2,1)S(1)}, bf16[64,32,128]{2,1,0:T(8,128)(2,1)}, u32[]{:S(2)}) %copy-start.1) | copy-done | bytes 524312
  1.0 1.1 %shard_map.47 = (bf16[32,64,128]{2,1,0:T(8,128)(2,1)S(1)}, bf16[24,64,128]{2,1,0:T(8,128)(2,1)S(1)}, bf16[24,64,128]{2,1,0:T(8,128)(2,1)S(1)}, bf16[7,64,128]{2,1,0:T(8,128)(2,1)S(1)}) custom-call(bf16[64,32,128]{2,1,0:T(8,128)(2,1)S(1)} %copy-done.1), custom_call_target="tpu_custom_call" | custom-call | tf_op jit(solution)/shard_map/pallas_call | solution.py:307
  2.1 0.1 collective-permute-start
  2.2 4.6 %collective-permute-start.1 = (bf16[24,64,128]{2,1,0:T(8,128)(2,1)S(1)}, bf16[24,64,128]{2,1,0:T(8,128)(2,1)S(1)}, u32[]{:S(2)}, u32[]{:S(2)}) collective-permute-start(bf16[24,64,128]{2,1,0:T(8,128)(2,1)S(1)} %get-tuple-element.20), channel_id=1, source_target_pairs={{2,4},{3,5},{4,2},{5,3},{6,8},{7,9},{8,6},{9,7},{10,12},{11,13},{1... | collective-permute-start | bytes 1179656 | tf_op jit(solution)/shard_map/ppermute | solution.py:326
  6.8 1.3 %collective-permute-start.2 = (bf16[7,64,128]{2,1,0:T(8,128)(2,1)S(1)}, bf16[7,64,128]{2,1,0:T(8,128)(2,1)S(1)}, u32[]{:S(2)}, u32[]{:S(2)}) collective-permute-start(bf16[7,64,128]{2,1,0:T(8,128)(2,1)S(1)} %get-tuple-element.21), channel_id=1, source_target_pairs={{0,1},{1,0},{2,3},{3,2},{4,5},{5,4},{6,7},{7,6},{8,9},{9,8},{10,11... | collective-permute-start | bytes 344072 | tf_op jit(solution)/shard_map/ppermute | solution.py:326
  8.0 2.4 %collective-permute-done.2.c_ref = bf16[7,64,128]{2,1,0:T(8,128)(2,1)S(1)} collective-permute-done((bf16[7,64,128]{2,1,0:T(8,128)(2,1)S(1)}, bf16[7,64,128]{2,1,0:T(8,128)(2,1)S(1)}, u32[]{:S(2)}, u32[]{:S(2)}) %collective-permute-start.2) | collective-permute-done | bytes 114720 | tf_op jit(solution)/shard_map/ppermute | solution.py:326
  10.5 3.6 %collective-permute-start.4 = (bf16[7,64,128]{2,1,0:T(8,128)(2,1)S(1)}, bf16[7,64,128]{2,1,0:T(8,128)(2,1)S(1)}, u32[]{:S(2)}, u32[]{:S(2)}) collective-permute-start(bf16[7,64,128]{2,1,0:T(8,128)(2,1)S(1)} %collective-permute-done.2.c_ref), channel_id=1, source_target_pairs={{2,4},{3,5},{4,2},{5,3},{6,8},{7,9},{8,6},{9,7},{10,12},{11,13},{1... | collective-permute-start | bytes 344072 | tf_op jit(solution)/shard_map/ppermute | solution.py:326
  14.1 0.1 collective-permute-start.3
  14.2 0.0 copy-start
  14.2 1.2 %copy-done = bf16[6,3,3,64,64]{4,3,2,1,0:T(8,128)(2,1)S(1)} copy-done((bf16[6,3,3,64,64]{4,3,2,1,0:T(8,128)(2,1)S(1)}, bf16[6,3,3,64,64]{4,3,2,1,0:T(8,128)(2,1)}, u32[]{:S(2)}) %copy-start) | copy-done | bytes 442392
  15.4 0.5 shard_map.46.w_ref
  15.9 0.0 copy-start.3
  15.9 0.6 collective-permute-done.4.e_ref
  16.6 0.0 collective-permute-done.3.d_ref
  16.6 9.0 %shard_map.48 = (bf16[32,64,128]{2,1,0:T(8,128)(2,1)S(1)}, bf16[32,16,128]{2,1,0:T(8,128)(2,1)S(1)}, bf16[32,16,128]{2,1,0:T(8,128)(2,1)S(1)}, bf16[32,16,128]{2,1,0:T(8,128)(2,1)S(1)}, bf16[32,16,128]{2,1,0:T(8,128)(2,1)S(1)}) custom-call(s32[6]{0:T(128)S(1)} %copy-done.3, bf16[6,192,208]{2,1,0:T(8,128)(2,1)S(1)} %shard_map.46.w_ref, ...), custom_call_target="tpu_custom_call" | custom-call | tf_op jit(solution)/shard_map/pallas_call | solution.py:307
  25.6 1.3 %collective-permute-start.5 = (bf16[32,16,128]{2,1,0:T(8,128)(2,1)S(1)}, bf16[32,16,128]{2,1,0:T(8,128)(2,1)S(1)}, u32[]{:S(2)}, u32[]{:S(2)}) collective-permute-start(bf16[32,16,128]{2,1,0:T(8,128)(2,1)S(1)} %get-tuple-element.23.own), channel_id=1, source_target_pairs={{1,0},{3,2},{5,4},{7,6},{8,9},{10,11},{12,13},{14,15},{17,16},{19,... | collective-permute-start | bytes 393224 | tf_op jit(solution)/shard_map/ppermute | solution.py:341
  26.9 0.1 collective-permute-start.7
  27.0 2.7 %collective-permute-start.8 = (bf16[32,16,128]{2,1,0:T(8,128)(2,1)S(1)}, bf16[32,16,128]{2,1,0:T(8,128)(2,1)S(1)}, u32[]{:S(2)}, u32[]{:S(2)}) collective-permute-start(bf16[32,16,128]{2,1,0:T(8,128)(2,1)S(1)} %get-tuple-element.25), channel_id=1, source_target_pairs={{0,4},{1,12},{2,6},{3,14},{4,0},{5,8},{6,2},{7,10},{8,5},{9,13},{1... | collective-permute-start | bytes 393224 | tf_op jit(solution)/shard_map/ppermute | solution.py:341
  29.7 0.0 collective-permute-start.9
  29.8 3.2 %collective-permute-done.5 = bf16[32,16,128]{2,1,0:T(8,128)(2,1)S(1)} collective-permute-done((bf16[32,16,128]{2,1,0:T(8,128)(2,1)S(1)}, bf16[32,16,128]{2,1,0:T(8,128)(2,1)S(1)}, u32[]{:S(2)}, u32[]{:S(2)}) %collective-permute-start.5) | collective-permute-done | bytes 131104 | tf_op jit(solution)/shard_map/ppermute | solution.py:341
  33.0 4.4 %collective-permute-start.6 = (bf16[32,16,128]{2,1,0:T(8,128)(2,1)S(1)}, bf16[32,16,128]{2,1,0:T(8,128)(2,1)S(1)}, u32[]{:S(2)}, u32[]{:S(2)}) collective-permute-start(bf16[32,16,128]{2,1,0:T(8,128)(2,1)S(1)} %collective-permute-done.5), channel_id=1, source_target_pairs={{0,8},{2,10},{4,12},{6,14},{9,1},{11,3},{13,5},{15,7},{16,24},{18,... | collective-permute-start | bytes 393224 | tf_op jit(solution)/shard_map/ppermute | solution.py:341
  37.5 0.2 collective-permute-done.9.m3
  37.7 2.1 %collective-permute-done.6.m0 = bf16[32,16,128]{2,1,0:T(8,128)(2,1)S(1)} collective-permute-done((bf16[32,16,128]{2,1,0:T(8,128)(2,1)S(1)}, bf16[32,16,128]{2,1,0:T(8,128)(2,1)S(1)}, u32[]{:S(2)}, u32[]{:S(2)}) %collective-permute-start.6) | collective-permute-done | bytes 131104 | tf_op jit(solution)/shard_map/ppermute | solution.py:341
  39.8 0.6 shard_map.49
  40.4 1.4 %collective-permute-start.10 = (bf16[24,64,128]{2,1,0:T(8,128)(2,1)S(1)}, bf16[24,64,128]{2,1,0:T(8,128)(2,1)S(1)}, u32[]{:S(2)}, u32[]{:S(2)}) collective-permute-start(bf16[24,64,128]{2,1,0:T(8,128)(2,1)S(1)} %get-tuple-element.28), channel_id=1, source_target_pairs={{0,2},{1,3},{2,0},{3,1},{4,6},{5,7},{6,4},{7,5},{8,10},{9,11},{10,... | collective-permute-start | bytes 1179656 | tf_op jit(solution)/shard_map/ppermute | solution.py:326
  41.9 5.8 %collective-permute-start.11 = (bf16[24,64,128]{2,1,0:T(8,128)(2,1)S(1)}, bf16[24,64,128]{2,1,0:T(8,128)(2,1)S(1)}, u32[]{:S(2)}, u32[]{:S(2)}) collective-permute-start(bf16[24,64,128]{2,1,0:T(8,128)(2,1)S(1)} %get-tuple-element.29), channel_id=1, source_target_pairs={{2,4},{3,5},{4,2},{5,3},{6,8},{7,9},{8,6},{9,7},{10,12},{11,13},{1... | collective-permute-start | bytes 1179656 | tf_op jit(solution)/shard_map/ppermute | solution.py:326
  47.7 7.2 %collective-permute-start.12 = (bf16[7,64,128]{2,1,0:T(8,128)(2,1)S(1)}, bf16[7,64,128]{2,1,0:T(8,128)(2,1)S(1)}, u32[]{:S(2)}, u32[]{:S(2)}) collective-permute-start(bf16[7,64,128]{2,1,0:T(8,128)(2,1)S(1)} %get-tuple-element.30), channel_id=1, source_target_pairs={{0,1},{1,0},{2,3},{3,2},{4,5},{5,4},{6,7},{7,6},{8,9},{9,8},{10,11... | collective-permute-start | bytes 344072 | tf_op jit(solution)/shard_map/ppermute | solution.py:326
  54.9 2.2 %collective-permute-done.12.c_ref = bf16[7,64,128]{2,1,0:T(8,128)(2,1)S(1)} collective-permute-done((bf16[7,64,128]{2,1,0:T(8,128)(2,1)S(1)}, bf16[7,64,128]{2,1,0:T(8,128)(2,1)S(1)}, u32[]{:S(2)}, u32[]{:S(2)}) %collective-permute-start.12) | collective-permute-done | bytes 114720 | tf_op jit(solution)/shard_map/ppermute | solution.py:326
  57.1 3.0 %collective-permute-start.14 = (bf16[7,64,128]{2,1,0:T(8,128)(2,1)S(1)}, bf16[7,64,128]{2,1,0:T(8,128)(2,1)S(1)}, u32[]{:S(2)}, u32[]{:S(2)}) collective-permute-start(bf16[7,64,128]{2,1,0:T(8,128)(2,1)S(1)} %collective-permute-done.12.c_ref), channel_id=1, source_target_pairs={{2,4},{3,5},{4,2},{5,3},{6,8},{7,9},{8,6},{9,7},{10,12},{11,13},{1... | collective-permute-start | bytes 344072 | tf_op jit(solution)/shard_map/ppermute | solution.py:326
  60.1 0.1 collective-permute-start.13
  60.2 3.0 %collective-permute-done.14.e_ref = bf16[7,64,128]{2,1,0:T(8,128)(2,1)S(1)} collective-permute-done((bf16[7,64,128]{2,1,0:T(8,128)(2,1)S(1)}, bf16[7,64,128]{2,1,0:T(8,128)(2,1)S(1)}, u32[]{:S(2)}, u32[]{:S(2)}) %collective-permute-start.14) | collective-permute-done | bytes 114720 | tf_op jit(solution)/shard_map/ppermute | solution.py:326
  63.2 8.9 %shard_map.50 = bf16[64,32,128]{2,1,0:T(8,128)(2,1)} custom-call(s32[6]{0:T(128)S(1)} %copy-done.3, bf16[6,192,208]{2,1,0:T(8,128)(2,1)S(1)} %shard_map.46.w_ref, bf16[32,64,128]{2,1,0:T(8,128)(2,1)S(1)} %get-tuple-element.27.xt_ref, bf16[24,64,128]{2,1,0:T(8,128)(2,1)S(1)} %collective-permute-done.10.a_ref, ...), custom_call_target="tpu_custom_call" | custom-call | tf_op jit(solution)/shard_map/pallas_call | solution.py:307
  (11 shorter events, 0.0 us)
Async XLA Ops:
  0.0 1.0 %copy-start.1 = (bf16[64,32,128]{2,1,0:T(8,128)(2,1)S(1)}, bf16[64,32,128]{2,1,0:T(8,128)(2,1)}, u32[]{:S(2)}) copy-start(bf16[64,32,128]{2,1,0:T(8,128)(2,1)} %x_ref.1) | copy-start | bytes 1572868
  2.1 12.1 %copy-start.2 = (bf16[6,64]{1,0:T(8,128)(2,1)S(1)}, bf16[6,64]{1,0:T(8,128)(2,1)}, u32[]{:S(2)}) copy-start(bf16[6,64]{1,0:T(8,128)(2,1)} %bias_ref.1) | copy-start | bytes 2308
  2.1 14.5 %collective-permute-start = (bf16[24,64,128]{2,1,0:T(8,128)(2,1)S(1)}, bf16[24,64,128]{2,1,0:T(8,128)(2,1)S(1)}, u32[]{:S(2)}, u32[]{:S(2)}) collective-permute-start(bf16[24,64,128]{2,1,0:T(8,128)(2,1)S(1)} %get-tuple-element.19), channel_id=1, source_target_pairs={{0,2},{1,3},{2,0},{3,1},{4,6},{5,7},{6,4},{7,5},{8,10},{9,11},{10,... | collective-permute-start | bytes 1179656 | tf_op jit(solution)/shard_map/ppermute | solution.py:326
  2.2 14.4 %collective-permute-start.1 = (bf16[24,64,128]{2,1,0:T(8,128)(2,1)S(1)}, bf16[24,64,128]{2,1,0:T(8,128)(2,1)S(1)}, u32[]{:S(2)}, u32[]{:S(2)}) collective-permute-start(bf16[24,64,128]{2,1,0:T(8,128)(2,1)S(1)} %get-tuple-element.20), channel_id=1, source_target_pairs={{2,4},{3,5},{4,2},{5,3},{6,8},{7,9},{8,6},{9,7},{10,12},{11,13},{1... | collective-permute-start | bytes 1179656 | tf_op jit(solution)/shard_map/ppermute | solution.py:326
  6.8 3.7 %collective-permute-start.2 = (bf16[7,64,128]{2,1,0:T(8,128)(2,1)S(1)}, bf16[7,64,128]{2,1,0:T(8,128)(2,1)S(1)}, u32[]{:S(2)}, u32[]{:S(2)}) collective-permute-start(bf16[7,64,128]{2,1,0:T(8,128)(2,1)S(1)} %get-tuple-element.21), channel_id=1, source_target_pairs={{0,1},{1,0},{2,3},{3,2},{4,5},{5,4},{6,7},{7,6},{8,9},{9,8},{10,11... | collective-permute-start | bytes 344072 | tf_op jit(solution)/shard_map/ppermute | solution.py:326
  10.5 6.1 %collective-permute-start.4 = (bf16[7,64,128]{2,1,0:T(8,128)(2,1)S(1)}, bf16[7,64,128]{2,1,0:T(8,128)(2,1)S(1)}, u32[]{:S(2)}, u32[]{:S(2)}) collective-permute-start(bf16[7,64,128]{2,1,0:T(8,128)(2,1)S(1)} %collective-permute-done.2.c_ref), channel_id=1, source_target_pairs={{2,4},{3,5},{4,2},{5,3},{6,8},{7,9},{8,6},{9,7},{10,12},{11,13},{1... | collective-permute-start | bytes 344072 | tf_op jit(solution)/shard_map/ppermute | solution.py:326
  14.1 2.5 %collective-permute-start.3 = (bf16[7,64,128]{2,1,0:T(8,128)(2,1)S(1)}, bf16[7,64,128]{2,1,0:T(8,128)(2,1)S(1)}, u32[]{:S(2)}, u32[]{:S(2)}) collective-permute-start(bf16[7,64,128]{2,1,0:T(8,128)(2,1)S(1)} %collective-permute-done.2.c_ref), channel_id=1, source_target_pairs={{0,2},{1,3},{2,0},{3,1},{4,6},{5,7},{6,4},{7,5},{8,10},{9,11},{10,... | collective-permute-start | bytes 344072 | tf_op jit(solution)/shard_map/ppermute | solution.py:326
  14.2 1.2 %copy-start = (bf16[6,3,3,64,64]{4,3,2,1,0:T(8,128)(2,1)S(1)}, bf16[6,3,3,64,64]{4,3,2,1,0:T(8,128)(2,1)}, u32[]{:S(2)}) copy-start(bf16[6,3,3,64,64]{4,3,2,1,0:T(8,128)(2,1)} %w_ref.1) | copy-start | bytes 1327108
  15.9 0.7 copy-start.3
  25.6 7.4 %collective-permute-start.5 = (bf16[32,16,128]{2,1,0:T(8,128)(2,1)S(1)}, bf16[32,16,128]{2,1,0:T(8,128)(2,1)S(1)}, u32[]{:S(2)}, u32[]{:S(2)}) collective-permute-start(bf16[32,16,128]{2,1,0:T(8,128)(2,1)S(1)} %get-tuple-element.23.own), channel_id=1, source_target_pairs={{1,0},{3,2},{5,4},{7,6},{8,9},{10,11},{12,13},{14,15},{17,16},{19,... | collective-permute-start | bytes 393224 | tf_op jit(solution)/shard_map/ppermute | solution.py:341
  26.9 10.6 %collective-permute-start.7 = (bf16[32,16,128]{2,1,0:T(8,128)(2,1)S(1)}, bf16[32,16,128]{2,1,0:T(8,128)(2,1)S(1)}, u32[]{:S(2)}, u32[]{:S(2)}) collective-permute-start(bf16[32,16,128]{2,1,0:T(8,128)(2,1)S(1)} %get-tuple-element.24), channel_id=1, source_target_pairs={{0,2},{1,10},{2,0},{3,8},{4,6},{5,14},{6,4},{7,12},{8,3},{9,11},{1... | collective-permute-start | bytes 393224 | tf_op jit(solution)/shard_map/ppermute | solution.py:341
  27.0 10.5 %collective-permute-start.8 = (bf16[32,16,128]{2,1,0:T(8,128)(2,1)S(1)}, bf16[32,16,128]{2,1,0:T(8,128)(2,1)S(1)}, u32[]{:S(2)}, u32[]{:S(2)}) collective-permute-start(bf16[32,16,128]{2,1,0:T(8,128)(2,1)S(1)} %get-tuple-element.25), channel_id=1, source_target_pairs={{0,4},{1,12},{2,6},{3,14},{4,0},{5,8},{6,2},{7,10},{8,5},{9,13},{1... | collective-permute-start | bytes 393224 | tf_op jit(solution)/shard_map/ppermute | solution.py:341
  29.7 7.9 %collective-permute-start.9 = (bf16[32,16,128]{2,1,0:T(8,128)(2,1)S(1)}, bf16[32,16,128]{2,1,0:T(8,128)(2,1)S(1)}, u32[]{:S(2)}, u32[]{:S(2)}) collective-permute-start(bf16[32,16,128]{2,1,0:T(8,128)(2,1)S(1)} %get-tuple-element.26), channel_id=1, source_target_pairs={{0,6},{1,14},{2,4},{3,12},{4,2},{5,10},{6,0},{7,8},{8,7},{9,15},{1... | collective-permute-start | bytes 393224 | tf_op jit(solution)/shard_map/ppermute | solution.py:341
  33.0 6.7 %collective-permute-start.6 = (bf16[32,16,128]{2,1,0:T(8,128)(2,1)S(1)}, bf16[32,16,128]{2,1,0:T(8,128)(2,1)S(1)}, u32[]{:S(2)}, u32[]{:S(2)}) collective-permute-start(bf16[32,16,128]{2,1,0:T(8,128)(2,1)S(1)} %collective-permute-done.5), channel_id=1, source_target_pairs={{0,8},{2,10},{4,12},{6,14},{9,1},{11,3},{13,5},{15,7},{16,24},{18,... | collective-permute-start | bytes 393224 | tf_op jit(solution)/shard_map/ppermute | solution.py:341
  40.4 22.7 %collective-permute-start.10 = (bf16[24,64,128]{2,1,0:T(8,128)(2,1)S(1)}, bf16[24,64,128]{2,1,0:T(8,128)(2,1)S(1)}, u32[]{:S(2)}, u32[]{:S(2)}) collective-permute-start(bf16[24,64,128]{2,1,0:T(8,128)(2,1)S(1)} %get-tuple-element.28), channel_id=1, source_target_pairs={{0,2},{1,3},{2,0},{3,1},{4,6},{5,7},{6,4},{7,5},{8,10},{9,11},{10,... | collective-permute-start | bytes 1179656 | tf_op jit(solution)/shard_map/ppermute | solution.py:326
  41.9 21.3 %collective-permute-start.11 = (bf16[24,64,128]{2,1,0:T(8,128)(2,1)S(1)}, bf16[24,64,128]{2,1,0:T(8,128)(2,1)S(1)}, u32[]{:S(2)}, u32[]{:S(2)}) collective-permute-start(bf16[24,64,128]{2,1,0:T(8,128)(2,1)S(1)} %get-tuple-element.29), channel_id=1, source_target_pairs={{2,4},{3,5},{4,2},{5,3},{6,8},{7,9},{8,6},{9,7},{10,12},{11,13},{1... | collective-permute-start | bytes 1179656 | tf_op jit(solution)/shard_map/ppermute | solution.py:326
  47.7 9.4 %collective-permute-start.12 = (bf16[7,64,128]{2,1,0:T(8,128)(2,1)S(1)}, bf16[7,64,128]{2,1,0:T(8,128)(2,1)S(1)}, u32[]{:S(2)}, u32[]{:S(2)}) collective-permute-start(bf16[7,64,128]{2,1,0:T(8,128)(2,1)S(1)} %get-tuple-element.30), channel_id=1, source_target_pairs={{0,1},{1,0},{2,3},{3,2},{4,5},{5,4},{6,7},{7,6},{8,9},{9,8},{10,11... | collective-permute-start | bytes 344072 | tf_op jit(solution)/shard_map/ppermute | solution.py:326
  57.1 6.1 %collective-permute-start.14 = (bf16[7,64,128]{2,1,0:T(8,128)(2,1)S(1)}, bf16[7,64,128]{2,1,0:T(8,128)(2,1)S(1)}, u32[]{:S(2)}, u32[]{:S(2)}) collective-permute-start(bf16[7,64,128]{2,1,0:T(8,128)(2,1)S(1)} %collective-permute-done.12.c_ref), channel_id=1, source_target_pairs={{2,4},{3,5},{4,2},{5,3},{6,8},{7,9},{8,6},{9,7},{10,12},{11,13},{1... | collective-permute-start | bytes 344072 | tf_op jit(solution)/shard_map/ppermute | solution.py:326
  60.1 3.1 %collective-permute-start.13 = (bf16[7,64,128]{2,1,0:T(8,128)(2,1)S(1)}, bf16[7,64,128]{2,1,0:T(8,128)(2,1)S(1)}, u32[]{:S(2)}, u32[]{:S(2)}) collective-permute-start(bf16[7,64,128]{2,1,0:T(8,128)(2,1)S(1)} %collective-permute-done.12.c_ref), channel_id=1, source_target_pairs={{0,2},{1,3},{2,0},{3,1},{4,6},{5,7},{6,4},{7,5},{8,10},{9,11},{10,... | collective-permute-start | bytes 344072 | tf_op jit(solution)/shard_map/ppermute | solution.py:326

commit v4 on v3

--- a/solution.py
+++ b/solution.py
@@ -173,9 +173,17 @@
     lane = lax.broadcasted_iota(jnp.int32, (CH, COLS), 1)
     ones = jnp.where(lax.broadcasted_iota(jnp.int32, (16, 2 * COLS), 0) == 0, 1.0, 0.0).astype(BF16)
     zeros = jnp.zeros((CH, 2 * COLS), BF16)
-    for i in range(HALO):
-        xb[i] = zeros
-        xb[FULL - HALO + i] = zeros
+
+    @pl.when(r == 0)
+    def _():
+        for i in range(HALO):
+            xb[i] = zeros
+
+    @pl.when(r == row_count - 1)
+    def _():
+        for i in range(HALO):
+            xb[FULL - HALO + i] = zeros
+
     src, dst = xa, xb
     for layer in range(HALF):
         s = dil_ref[base + layer]

time: 73.1 us -> 73.2 us (level)
  no operation moved by 1% of the time
where the time goes in v4:
time: 73.2 us; the launch traced here: 72.1 us
  starting transfers between devices  35.7 us (49%)
  Pallas kernels  20.2 us (28%)
  waiting for transfers between devices  13.8 us (19%)
  local copies, waits for them, and re-layouts  2.21 us (3%)
    ppermute x10, starting transfers between devices, swap(): return lax.ppermute(x, ('row', 'col'), perm)  27.1 us
    pallas_call x5, Pallas kernels, kernel_call(): pl.pallas_call(body, out_shape=[jax.ShapeDtypeStruct(shape, BF16) for sha...  20.2 us
    ppermute x5, starting transfers between devices, send(): lax.ppermute(x, ('row', 'col'), [(2 * r + c, 2 * target(r, c)[0] + target...  8.62 us
    ppermute x10, waiting for transfers between devices, swap(): return lax.ppermute(x, ('row', 'col'), perm)  8.32 us
    ppermute x5, waiting for transfers between devices, send(): lax.ppermute(x, ('row', 'col'), [(2 * r + c, 2 * target(r, c)[0] + target...  5.51 us
    unnamed x8, local copies, waits for them, and re-layouts  2.21 us
  transfers between devices with their start and end apart: 15, of which 7 were waited for; matrix products, arithmetic and copies ran while one was open for 0% of the time, Pallas kernels for 1%

profile of v4, /device:TPU:1, one launch (start us, length us, event | category | flops | bytes accessed | tf_op | source)
XLA Modules:
  0.0 72.1 jit_solution(16423609791597600557)
XLA Ops:
  0.0 1.0 %copy-done.1 = bf16[64,32,128]{2,1,0:T(8,128)(2,1)S(1)} copy-done((bf16[64,32,128]{2,1,0:T(8,128)(2,1)S(1)}, bf16[64,32,128]{2,1,0:T(8,128)(2,1)}, u32[]{:S(2)}) %copy-start.1) | copy-done | bytes 524312
  1.0 1.1 %shard_map.47 = (bf16[32,64,128]{2,1,0:T(8,128)(2,1)S(1)}, bf16[24,64,128]{2,1,0:T(8,128)(2,1)S(1)}, bf16[24,64,128]{2,1,0:T(8,128)(2,1)S(1)}, bf16[7,64,128]{2,1,0:T(8,128)(2,1)S(1)}) custom-call(bf16[64,32,128]{2,1,0:T(8,128)(2,1)S(1)} %copy-done.1), custom_call_target="tpu_custom_call" | custom-call | tf_op jit(solution)/shard_map/pallas_call | solution.py:315
  2.1 0.1 collective-permute-start
  2.2 4.6 %collective-permute-start.1 = (bf16[24,64,128]{2,1,0:T(8,128)(2,1)S(1)}, bf16[24,64,128]{2,1,0:T(8,128)(2,1)S(1)}, u32[]{:S(2)}, u32[]{:S(2)}) collective-permute-start(bf16[24,64,128]{2,1,0:T(8,128)(2,1)S(1)} %get-tuple-element.20), channel_id=1, source_target_pairs={{2,4},{3,5},{4,2},{5,3},{6,8},{7,9},{8,6},{9,7},{10,12},{11,13},{1... | collective-permute-start | bytes 1179656 | tf_op jit(solution)/shard_map/ppermute | solution.py:334
  6.8 1.3 %collective-permute-start.2 = (bf16[7,64,128]{2,1,0:T(8,128)(2,1)S(1)}, bf16[7,64,128]{2,1,0:T(8,128)(2,1)S(1)}, u32[]{:S(2)}, u32[]{:S(2)}) collective-permute-start(bf16[7,64,128]{2,1,0:T(8,128)(2,1)S(1)} %get-tuple-element.21), channel_id=1, source_target_pairs={{0,1},{1,0},{2,3},{3,2},{4,5},{5,4},{6,7},{7,6},{8,9},{9,8},{10,11... | collective-permute-start | bytes 344072 | tf_op jit(solution)/shard_map/ppermute | solution.py:334
  8.0 2.4 %collective-permute-done.2.c_ref = bf16[7,64,128]{2,1,0:T(8,128)(2,1)S(1)} collective-permute-done((bf16[7,64,128]{2,1,0:T(8,128)(2,1)S(1)}, bf16[7,64,128]{2,1,0:T(8,128)(2,1)S(1)}, u32[]{:S(2)}, u32[]{:S(2)}) %collective-permute-start.2) | collective-permute-done | bytes 114720 | tf_op jit(solution)/shard_map/ppermute | solution.py:334
  10.5 3.6 %collective-permute-start.4 = (bf16[7,64,128]{2,1,0:T(8,128)(2,1)S(1)}, bf16[7,64,128]{2,1,0:T(8,128)(2,1)S(1)}, u32[]{:S(2)}, u32[]{:S(2)}) collective-permute-start(bf16[7,64,128]{2,1,0:T(8,128)(2,1)S(1)} %collective-permute-done.2.c_ref), channel_id=1, source_target_pairs={{2,4},{3,5},{4,2},{5,3},{6,8},{7,9},{8,6},{9,7},{10,12},{11,13},{1... | collective-permute-start | bytes 344072 | tf_op jit(solution)/shard_map/ppermute | solution.py:334
  14.1 0.1 collective-permute-start.3
  14.2 0.0 copy-start
  14.2 1.2 %copy-done = bf16[6,3,3,64,64]{4,3,2,1,0:T(8,128)(2,1)S(1)} copy-done((bf16[6,3,3,64,64]{4,3,2,1,0:T(8,128)(2,1)S(1)}, bf16[6,3,3,64,64]{4,3,2,1,0:T(8,128)(2,1)}, u32[]{:S(2)}) %copy-start) | copy-done | bytes 442392
  15.4 0.5 shard_map.46.w_ref
  15.9 0.0 copy-start.3
  15.9 0.6 collective-permute-done.4.e_ref
  16.6 0.0 collective-permute-done.3.d_ref
  16.6 9.0 %shard_map.48 = (bf16[32,64,128]{2,1,0:T(8,128)(2,1)S(1)}, bf16[32,16,128]{2,1,0:T(8,128)(2,1)S(1)}, bf16[32,16,128]{2,1,0:T(8,128)(2,1)S(1)}, bf16[32,16,128]{2,1,0:T(8,128)(2,1)S(1)}, bf16[32,16,128]{2,1,0:T(8,128)(2,1)S(1)}) custom-call(s32[6]{0:T(128)S(1)} %copy-done.3, bf16[6,192,208]{2,1,0:T(8,128)(2,1)S(1)} %shard_map.46.w_ref, ...), custom_call_target="tpu_custom_call" | custom-call | tf_op jit(solution)/shard_map/pallas_call | solution.py:315
  25.6 1.3 %collective-permute-start.5 = (bf16[32,16,128]{2,1,0:T(8,128)(2,1)S(1)}, bf16[32,16,128]{2,1,0:T(8,128)(2,1)S(1)}, u32[]{:S(2)}, u32[]{:S(2)}) collective-permute-start(bf16[32,16,128]{2,1,0:T(8,128)(2,1)S(1)} %get-tuple-element.23.own), channel_id=1, source_target_pairs={{1,0},{3,2},{5,4},{7,6},{8,9},{10,11},{12,13},{14,15},{17,16},{19,... | collective-permute-start | bytes 393224 | tf_op jit(solution)/shard_map/ppermute | solution.py:349
  26.9 0.1 collective-permute-start.7
  27.0 2.7 %collective-permute-start.8 = (bf16[32,16,128]{2,1,0:T(8,128)(2,1)S(1)}, bf16[32,16,128]{2,1,0:T(8,128)(2,1)S(1)}, u32[]{:S(2)}, u32[]{:S(2)}) collective-permute-start(bf16[32,16,128]{2,1,0:T(8,128)(2,1)S(1)} %get-tuple-element.25), channel_id=1, source_target_pairs={{0,4},{1,12},{2,6},{3,14},{4,0},{5,8},{6,2},{7,10},{8,5},{9,13},{1... | collective-permute-start | bytes 393224 | tf_op jit(solution)/shard_map/ppermute | solution.py:349
  29.7 0.0 collective-permute-start.9
  29.8 3.2 %collective-permute-done.5 = bf16[32,16,128]{2,1,0:T(8,128)(2,1)S(1)} collective-permute-done((bf16[32,16,128]{2,1,0:T(8,128)(2,1)S(1)}, bf16[32,16,128]{2,1,0:T(8,128)(2,1)S(1)}, u32[]{:S(2)}, u32[]{:S(2)}) %collective-permute-start.5) | collective-permute-done | bytes 131104 | tf_op jit(solution)/shard_map/ppermute | solution.py:349
  33.0 4.5 %collective-permute-start.6 = (bf16[32,16,128]{2,1,0:T(8,128)(2,1)S(1)}, bf16[32,16,128]{2,1,0:T(8,128)(2,1)S(1)}, u32[]{:S(2)}, u32[]{:S(2)}) collective-permute-start(bf16[32,16,128]{2,1,0:T(8,128)(2,1)S(1)} %collective-permute-done.5), channel_id=1, source_target_pairs={{0,8},{2,10},{4,12},{6,14},{9,1},{11,3},{13,5},{15,7},{16,24},{18,... | collective-permute-start | bytes 393224 | tf_op jit(solution)/shard_map/ppermute | solution.py:349
  37.5 0.2 collective-permute-done.9.m3
  37.7 2.1 %collective-permute-done.6.m0 = bf16[32,16,128]{2,1,0:T(8,128)(2,1)S(1)} collective-permute-done((bf16[32,16,128]{2,1,0:T(8,128)(2,1)S(1)}, bf16[32,16,128]{2,1,0:T(8,128)(2,1)S(1)}, u32[]{:S(2)}, u32[]{:S(2)}) %collective-permute-start.6) | collective-permute-done | bytes 131104 | tf_op jit(solution)/shard_map/ppermute | solution.py:349
  39.8 0.6 shard_map.49
  40.5 1.4 %collective-permute-start.10 = (bf16[24,64,128]{2,1,0:T(8,128)(2,1)S(1)}, bf16[24,64,128]{2,1,0:T(8,128)(2,1)S(1)}, u32[]{:S(2)}, u32[]{:S(2)}) collective-permute-start(bf16[24,64,128]{2,1,0:T(8,128)(2,1)S(1)} %get-tuple-element.28), channel_id=1, source_target_pairs={{0,2},{1,3},{2,0},{3,1},{4,6},{5,7},{6,4},{7,5},{8,10},{9,11},{10,... | collective-permute-start | bytes 1179656 | tf_op jit(solution)/shard_map/ppermute | solution.py:334
  41.9 5.8 %collective-permute-start.11 = (bf16[24,64,128]{2,1,0:T(8,128)(2,1)S(1)}, bf16[24,64,128]{2,1,0:T(8,128)(2,1)S(1)}, u32[]{:S(2)}, u32[]{:S(2)}) collective-permute-start(bf16[24,64,128]{2,1,0:T(8,128)(2,1)S(1)} %get-tuple-element.29), channel_id=1, source_target_pairs={{2,4},{3,5},{4,2},{5,3},{6,8},{7,9},{8,6},{9,7},{10,12},{11,13},{1... | collective-permute-start | bytes 1179656 | tf_op jit(solution)/shard_map/ppermute | solution.py:334
  47.7 7.2 %collective-permute-start.12 = (bf16[7,64,128]{2,1,0:T(8,128)(2,1)S(1)}, bf16[7,64,128]{2,1,0:T(8,128)(2,1)S(1)}, u32[]{:S(2)}, u32[]{:S(2)}) collective-permute-start(bf16[7,64,128]{2,1,0:T(8,128)(2,1)S(1)} %get-tuple-element.30), channel_id=1, source_target_pairs={{0,1},{1,0},{2,3},{3,2},{4,5},{5,4},{6,7},{7,6},{8,9},{9,8},{10,11... | collective-permute-start | bytes 344072 | tf_op jit(solution)/shard_map/ppermute | solution.py:334
  54.9 2.2 %collective-permute-done.12.c_ref = bf16[7,64,128]{2,1,0:T(8,128)(2,1)S(1)} collective-permute-done((bf16[7,64,128]{2,1,0:T(8,128)(2,1)S(1)}, bf16[7,64,128]{2,1,0:T(8,128)(2,1)S(1)}, u32[]{:S(2)}, u32[]{:S(2)}) %collective-permute-start.12) | collective-permute-done | bytes 114720 | tf_op jit(solution)/shard_map/ppermute | solution.py:334
  57.0 3.0 %collective-permute-start.14 = (bf16[7,64,128]{2,1,0:T(8,128)(2,1)S(1)}, bf16[7,64,128]{2,1,0:T(8,128)(2,1)S(1)}, u32[]{:S(2)}, u32[]{:S(2)}) collective-permute-start(bf16[7,64,128]{2,1,0:T(8,128)(2,1)S(1)} %collective-permute-done.12.c_ref), channel_id=1, source_target_pairs={{2,4},{3,5},{4,2},{5,3},{6,8},{7,9},{8,6},{9,7},{10,12},{11,13},{1... | collective-permute-start | bytes 344072 | tf_op jit(solution)/shard_map/ppermute | solution.py:334
  60.0 0.1 collective-permute-start.13
  60.1 3.0 %collective-permute-done.14.e_ref = bf16[7,64,128]{2,1,0:T(8,128)(2,1)S(1)} collective-permute-done((bf16[7,64,128]{2,1,0:T(8,128)(2,1)S(1)}, bf16[7,64,128]{2,1,0:T(8,128)(2,1)S(1)}, u32[]{:S(2)}, u32[]{:S(2)}) %collective-permute-start.14) | collective-permute-done | bytes 114720 | tf_op jit(solution)/shard_map/ppermute | solution.py:334
  63.2 8.9 %shard_map.50 = bf16[64,32,128]{2,1,0:T(8,128)(2,1)} custom-call(s32[6]{0:T(128)S(1)} %copy-done.3, bf16[6,192,208]{2,1,0:T(8,128)(2,1)S(1)} %shard_map.46.w_ref, bf16[32,64,128]{2,1,0:T(8,128)(2,1)S(1)} %get-tuple-element.27.xt_ref, bf16[24,64,128]{2,1,0:T(8,128)(2,1)S(1)} %collective-permute-done.10.a_ref, ...), custom_call_target="tpu_custom_call" | custom-call | tf_op jit(solution)/shard_map/pallas_call | solution.py:315
  (11 shorter events, 0.0 us)
Async XLA Ops:
  0.0 1.0 %copy-start.1 = (bf16[64,32,128]{2,1,0:T(8,128)(2,1)S(1)}, bf16[64,32,128]{2,1,0:T(8,128)(2,1)}, u32[]{:S(2)}) copy-start(bf16[64,32,128]{2,1,0:T(8,128)(2,1)} %x_ref.1) | copy-start | bytes 1572868
  2.1 12.1 %copy-start.2 = (bf16[6,64]{1,0:T(8,128)(2,1)S(1)}, bf16[6,64]{1,0:T(8,128)(2,1)}, u32[]{:S(2)}) copy-start(bf16[6,64]{1,0:T(8,128)(2,1)} %bias_ref.1) | copy-start | bytes 2308
  2.1 14.5 %collective-permute-start = (bf16[24,64,128]{2,1,0:T(8,128)(2,1)S(1)}, bf16[24,64,128]{2,1,0:T(8,128)(2,1)S(1)}, u32[]{:S(2)}, u32[]{:S(2)}) collective-permute-start(bf16[24,64,128]{2,1,0:T(8,128)(2,1)S(1)} %get-tuple-element.19), channel_id=1, source_target_pairs={{0,2},{1,3},{2,0},{3,1},{4,6},{5,7},{6,4},{7,5},{8,10},{9,11},{10,... | collective-permute-start | bytes 1179656 | tf_op jit(solution)/shard_map/ppermute | solution.py:334
  2.2 14.4 %collective-permute-start.1 = (bf16[24,64,128]{2,1,0:T(8,128)(2,1)S(1)}, bf16[24,64,128]{2,1,0:T(8,128)(2,1)S(1)}, u32[]{:S(2)}, u32[]{:S(2)}) collective-permute-start(bf16[24,64,128]{2,1,0:T(8,128)(2,1)S(1)} %get-tuple-element.20), channel_id=1, source_target_pairs={{2,4},{3,5},{4,2},{5,3},{6,8},{7,9},{8,6},{9,7},{10,12},{11,13},{1... | collective-permute-start | bytes 1179656 | tf_op jit(solution)/shard_map/ppermute | solution.py:334
  6.8 3.7 %collective-permute-start.2 = (bf16[7,64,128]{2,1,0:T(8,128)(2,1)S(1)}, bf16[7,64,128]{2,1,0:T(8,128)(2,1)S(1)}, u32[]{:S(2)}, u32[]{:S(2)}) collective-permute-start(bf16[7,64,128]{2,1,0:T(8,128)(2,1)S(1)} %get-tuple-element.21), channel_id=1, source_target_pairs={{0,1},{1,0},{2,3},{3,2},{4,5},{5,4},{6,7},{7,6},{8,9},{9,8},{10,11... | collective-permute-start | bytes 344072 | tf_op jit(solution)/shard_map/ppermute | solution.py:334
  10.5 6.1 %collective-permute-start.4 = (bf16[7,64,128]{2,1,0:T(8,128)(2,1)S(1)}, bf16[7,64,128]{2,1,0:T(8,128)(2,1)S(1)}, u32[]{:S(2)}, u32[]{:S(2)}) collective-permute-start(bf16[7,64,128]{2,1,0:T(8,128)(2,1)S(1)} %collective-permute-done.2.c_ref), channel_id=1, source_target_pairs={{2,4},{3,5},{4,2},{5,3},{6,8},{7,9},{8,6},{9,7},{10,12},{11,13},{1... | collective-permute-start | bytes 344072 | tf_op jit(solution)/shard_map/ppermute | solution.py:334
  14.1 2.5 %collective-permute-start.3 = (bf16[7,64,128]{2,1,0:T(8,128)(2,1)S(1)}, bf16[7,64,128]{2,1,0:T(8,128)(2,1)S(1)}, u32[]{:S(2)}, u32[]{:S(2)}) collective-permute-start(bf16[7,64,128]{2,1,0:T(8,128)(2,1)S(1)} %collective-permute-done.2.c_ref), channel_id=1, source_target_pairs={{0,2},{1,3},{2,0},{3,1},{4,6},{5,7},{6,4},{7,5},{8,10},{9,11},{10,... | collective-permute-start | bytes 344072 | tf_op jit(solution)/shard_map/ppermute | solution.py:334
  14.2 1.2 %copy-start = (bf16[6,3,3,64,64]{4,3,2,1,0:T(8,128)(2,1)S(1)}, bf16[6,3,3,64,64]{4,3,2,1,0:T(8,128)(2,1)}, u32[]{:S(2)}) copy-start(bf16[6,3,3,64,64]{4,3,2,1,0:T(8,128)(2,1)} %w_ref.1) | copy-start | bytes 1327108
  15.9 0.7 copy-start.3
  25.6 7.4 %collective-permute-start.5 = (bf16[32,16,128]{2,1,0:T(8,128)(2,1)S(1)}, bf16[32,16,128]{2,1,0:T(8,128)(2,1)S(1)}, u32[]{:S(2)}, u32[]{:S(2)}) collective-permute-start(bf16[32,16,128]{2,1,0:T(8,128)(2,1)S(1)} %get-tuple-element.23.own), channel_id=1, source_target_pairs={{1,0},{3,2},{5,4},{7,6},{8,9},{10,11},{12,13},{14,15},{17,16},{19,... | collective-permute-start | bytes 393224 | tf_op jit(solution)/shard_map/ppermute | solution.py:349
  26.9 10.6 %collective-permute-start.7 = (bf16[32,16,128]{2,1,0:T(8,128)(2,1)S(1)}, bf16[32,16,128]{2,1,0:T(8,128)(2,1)S(1)}, u32[]{:S(2)}, u32[]{:S(2)}) collective-permute-start(bf16[32,16,128]{2,1,0:T(8,128)(2,1)S(1)} %get-tuple-element.24), channel_id=1, source_target_pairs={{0,2},{1,10},{2,0},{3,8},{4,6},{5,14},{6,4},{7,12},{8,3},{9,11},{1... | collective-permute-start | bytes 393224 | tf_op jit(solution)/shard_map/ppermute | solution.py:349
  27.0 10.5 %collective-permute-start.8 = (bf16[32,16,128]{2,1,0:T(8,128)(2,1)S(1)}, bf16[32,16,128]{2,1,0:T(8,128)(2,1)S(1)}, u32[]{:S(2)}, u32[]{:S(2)}) collective-permute-start(bf16[32,16,128]{2,1,0:T(8,128)(2,1)S(1)} %get-tuple-element.25), channel_id=1, source_target_pairs={{0,4},{1,12},{2,6},{3,14},{4,0},{5,8},{6,2},{7,10},{8,5},{9,13},{1... | collective-permute-start | bytes 393224 | tf_op jit(solution)/shard_map/ppermute | solution.py:349
  29.7 7.9 %collective-permute-start.9 = (bf16[32,16,128]{2,1,0:T(8,128)(2,1)S(1)}, bf16[32,16,128]{2,1,0:T(8,128)(2,1)S(1)}, u32[]{:S(2)}, u32[]{:S(2)}) collective-permute-start(bf16[32,16,128]{2,1,0:T(8,128)(2,1)S(1)} %get-tuple-element.26), channel_id=1, source_target_pairs={{0,6},{1,14},{2,4},{3,12},{4,2},{5,10},{6,0},{7,8},{8,7},{9,15},{1... | collective-permute-start | bytes 393224 | tf_op jit(solution)/shard_map/ppermute | solution.py:349
  33.0 6.8 %collective-permute-start.6 = (bf16[32,16,128]{2,1,0:T(8,128)(2,1)S(1)}, bf16[32,16,128]{2,1,0:T(8,128)(2,1)S(1)}, u32[]{:S(2)}, u32[]{:S(2)}) collective-permute-start(bf16[32,16,128]{2,1,0:T(8,128)(2,1)S(1)} %collective-permute-done.5), channel_id=1, source_target_pairs={{0,8},{2,10},{4,12},{6,14},{9,1},{11,3},{13,5},{15,7},{16,24},{18,... | collective-permute-start | bytes 393224 | tf_op jit(solution)/shard_map/ppermute | solution.py:349
  40.5 22.7 %collective-permute-start.10 = (bf16[24,64,128]{2,1,0:T(8,128)(2,1)S(1)}, bf16[24,64,128]{2,1,0:T(8,128)(2,1)S(1)}, u32[]{:S(2)}, u32[]{:S(2)}) collective-permute-start(bf16[24,64,128]{2,1,0:T(8,128)(2,1)S(1)} %get-tuple-element.28), channel_id=1, source_target_pairs={{0,2},{1,3},{2,0},{3,1},{4,6},{5,7},{6,4},{7,5},{8,10},{9,11},{10,... | collective-permute-start | bytes 1179656 | tf_op jit(solution)/shard_map/ppermute | solution.py:334
  41.9 21.3 %collective-permute-start.11 = (bf16[24,64,128]{2,1,0:T(8,128)(2,1)S(1)}, bf16[24,64,128]{2,1,0:T(8,128)(2,1)S(1)}, u32[]{:S(2)}, u32[]{:S(2)}) collective-permute-start(bf16[24,64,128]{2,1,0:T(8,128)(2,1)S(1)} %get-tuple-element.29), channel_id=1, source_target_pairs={{2,4},{3,5},{4,2},{5,3},{6,8},{7,9},{8,6},{9,7},{10,12},{11,13},{1... | collective-permute-start | bytes 1179656 | tf_op jit(solution)/shard_map/ppermute | solution.py:334
  47.7 9.3 %collective-permute-start.12 = (bf16[7,64,128]{2,1,0:T(8,128)(2,1)S(1)}, bf16[7,64,128]{2,1,0:T(8,128)(2,1)S(1)}, u32[]{:S(2)}, u32[]{:S(2)}) collective-permute-start(bf16[7,64,128]{2,1,0:T(8,128)(2,1)S(1)} %get-tuple-element.30), channel_id=1, source_target_pairs={{0,1},{1,0},{2,3},{3,2},{4,5},{5,4},{6,7},{7,6},{8,9},{9,8},{10,11... | collective-permute-start | bytes 344072 | tf_op jit(solution)/shard_map/ppermute | solution.py:334
  57.0 6.1 %collective-permute-start.14 = (bf16[7,64,128]{2,1,0:T(8,128)(2,1)S(1)}, bf16[7,64,128]{2,1,0:T(8,128)(2,1)S(1)}, u32[]{:S(2)}, u32[]{:S(2)}) collective-permute-start(bf16[7,64,128]{2,1,0:T(8,128)(2,1)S(1)} %collective-permute-done.12.c_ref), channel_id=1, source_target_pairs={{2,4},{3,5},{4,2},{5,3},{6,8},{7,9},{8,6},{9,7},{10,12},{11,13},{1... | collective-permute-start | bytes 344072 | tf_op jit(solution)/shard_map/ppermute | solution.py:334
  60.0 3.1 %collective-permute-start.13 = (bf16[7,64,128]{2,1,0:T(8,128)(2,1)S(1)}, bf16[7,64,128]{2,1,0:T(8,128)(2,1)S(1)}, u32[]{:S(2)}, u32[]{:S(2)}) collective-permute-start(bf16[7,64,128]{2,1,0:T(8,128)(2,1)S(1)} %collective-permute-done.12.c_ref), channel_id=1, source_target_pairs={{0,2},{1,3},{2,0},{3,1},{4,6},{5,7},{6,4},{7,5},{8,10},{9,11},{10,... | collective-permute-start | bytes 344072 | tf_op jit(solution)/shard_map/ppermute | solution.py:334
